TPU v7x, 512 devices: a whole 4x8x8 slice. The times are simulated.
512 devices in a mesh: seq: 32 (over y_hi, z, core), chan: 16 (over x, y_lo).
Axes of the slice: x: 4, y: 8 (y_hi: 2, y_lo: 4; y = y_hi * 4 + y_lo), z: 8, core: 2. Of those that a mesh axis runs over, the one named last changes fastest.
Arguments:
- values: bfloat16 [4096, 1024], P('seq', 'chan'), may hold values from -6 to 6
- gate_inner: bfloat16 [4096, 1024], P('seq', 'chan'), may hold values from -6 to 6
- gate_outer: bfloat16 [4096, 1024], P('seq', 'chan'), may hold values from -6 to 6
- filter_one: float32 [16, 4096], P('chan', 'seq'), may hold values from -0.09375 to 0.09375
- filter_two: float32 [16, 4096], P('chan', 'seq'), may hold values from -0.09375 to 0.09375
- teacher: bfloat16 [4096, 1024], P('seq', 'chan'), may hold values from -6 to 6
- w_out: bfloat16 [1024, 1024], P(None, 'chan'), may hold values from -0.1875 to 0.1875
- gene_ids: int32 [4096], P('seq'), may hold values from 0 to 25425
- cell_lengths: int32 [4], replicated, may hold values from 1 to 2048, 4096 in all
- gene_weights: float32 [25426], replicated, may hold values from 0.5 to 2
Outputs:
- grad_values: bfloat16 [4096, 1024], P('seq', 'chan')
- grad_inner: bfloat16 [4096, 1024], P('seq', 'chan')
- grad_outer: bfloat16 [4096, 1024], P('seq', 'chan')
- grad_filter_one: float32 [16, 4096], P('chan', 'seq')
- grad_filter_two: float32 [16, 4096], P('chan', 'seq')
- grad_w_out: float32 [1024, 1024], P('seq', 'chan')
Inputs may be any that keep to these rules, and one draw needn't show every extreme that they name: `cell_lengths`: the lengths sum to 4096, and the largest equals 2048.
All inputs are finite; a program needn't handle non-finite values.
Results may differ from a plain program's by a relative error of at most 0.0051.
Values may be sent and summed in bfloat16 or wider, within the bound.
A program may use at most 64 MiB of HBM per device.

v0:
```python
import jax
import jax.numpy as jnp
from jax import lax
from jax.sharding import PartitionSpec as P

TWO_PI = 6.283185307179586
PRECISE = lax.Precision.HIGHEST


def phases(left_index, right_index, modulus):
    turn_count = left_index[:, None] * right_index[None, :] % modulus
    centred = jnp.where(2 * turn_count > modulus, turn_count - modulus, turn_count)
    radians = centred.astype(jnp.float32) * (TWO_PI / modulus)
    return (jnp.cos(radians), jnp.sin(radians))


def make_tables(length, shard_count, position):
    stride = length // shard_count
    lane_index = jnp.arange(shard_count, dtype=jnp.int32)
    doubled = jnp.arange(2 * shard_count, dtype=jnp.int32)
    padded_len = 2 * shard_count * length
    offsets = jnp.arange(length, dtype=jnp.int32)
    wide_cos, wide_sin = phases(lane_index, doubled, 2 * shard_count)
    near_cos, near_sin = phases(
        position * stride + jnp.arange(stride, dtype=jnp.int32), doubled, padded_len
    )
    far_cos, far_sin = phases(offsets, 2 * position + jnp.arange(2, dtype=jnp.int32), padded_len)
    long_cos, long_sin = phases(offsets, offsets, length)
    return (wide_cos, wide_sin, near_cos, near_sin, far_cos, far_sin, long_cos, long_sin)


def spread_out(packed):
    return lax.all_to_all(packed, "seq", split_axis=0, concat_axis=1, tiled=True)


def bring_back(packed):
    return lax.all_to_all(packed, "seq", split_axis=1, concat_axis=0, tiled=True)


def halves(packed):
    half_width = packed.shape[-1] // 2
    return (packed[..., :half_width], packed[..., half_width:])


def long_transform(real_in, imag_in, table_cos, table_sin, sign):
    shape_in = real_in.shape
    stacked = jnp.concatenate(
        [real_in.reshape(shape_in[0], -1), imag_in.reshape(shape_in[0], -1)], axis=1
    )
    cos_part = jnp.dot(table_cos, stacked, precision=PRECISE)
    sin_part = jnp.dot(table_sin, stacked, precision=PRECISE)
    cos_real, cos_imag = halves(cos_part)
    sin_real, sin_imag = halves(sin_part)
    real_out = cos_real + sign * sin_imag
    imag_out = cos_imag - sign * sin_real
    return (real_out.reshape(shape_in), imag_out.reshape(shape_in))


def forward_columns(columns, tables):
    wide_cos, wide_sin, near_cos, near_sin, far_cos, far_sin, long_cos, long_sin = tables
    real_part = jnp.einsum("rnf,nk->rkf", columns, wide_cos, precision=PRECISE)
    imag_part = -jnp.einsum("rnf,nk->rkf", columns, wide_sin, precision=PRECISE)
    twist_cos = near_cos[:, :, None]
    twist_sin = near_sin[:, :, None]
    turned = jnp.concatenate(
        [
            real_part * twist_cos + imag_part * twist_sin,
            imag_part * twist_cos - real_part * twist_sin,
        ],
        axis=2,
    )
    arrived_real, arrived_imag = halves(bring_back(turned))
    return long_transform(arrived_real, arrived_imag, long_cos, long_sin, 1.0)


def inverse_columns(spectra, tables):
    wide_cos, wide_sin, near_cos, near_sin, far_cos, far_sin, long_cos, long_sin = tables
    time_real, time_imag = long_transform(spectra[0], spectra[1], long_cos, long_sin, -1.0)
    twist_cos = far_cos[:, :, None]
    twist_sin = far_sin[:, :, None]
    turned = jnp.concatenate(
        [
            time_real * twist_cos - time_imag * twist_sin,
            time_imag * twist_cos + time_real * twist_sin,
        ],
        axis=2,
    )
    arrived_real, arrived_imag = halves(spread_out(turned))
    padded_len = 2 * wide_cos.shape[0] * spectra[0].shape[0]
    summed = jnp.einsum("rkf,nk->rnf", arrived_real, wide_cos, precision=PRECISE) - jnp.einsum(
        "rkf,nk->rnf", arrived_imag, wide_sin, precision=PRECISE
    )
    return summed * (1.0 / padded_len)


def spectrum(block_data, tables):
    return forward_columns(spread_out(block_data[:, None, :]), tables)


def signal_rows(spectra, tables):
    arrived = bring_back(inverse_columns(spectra, tables))
    return arrived.reshape(arrived.shape[0], -1)


def take_range(spectra, start, stop):
    return (spectra[0][..., start:stop], spectra[1][..., start:stop])


def joined(first_pair, second_pair):
    return (
        jnp.concatenate([first_pair[0], second_pair[0]], axis=-1),
        jnp.concatenate([first_pair[1], second_pair[1]], axis=-1),
    )


def filtered(spectra, filters, conjugate):
    groups = filters[0].shape[-1]
    shape_in = spectra[0].shape
    split_shape = shape_in[:-1] + (groups, shape_in[-1] // groups)
    left_real = spectra[0].reshape(split_shape)
    left_imag = spectra[1].reshape(split_shape)
    right_real = filters[0][..., None]
    right_imag = filters[1][..., None] * (-1.0 if conjugate else 1.0)
    out_real = left_real * right_real - left_imag * right_imag
    out_imag = left_real * right_imag + left_imag * right_real
    return (out_real.reshape(shape_in), out_imag.reshape(shape_in))


def pooled(first_pair, second_pair, groups):
    shape_in = first_pair[0].shape
    split_shape = shape_in[:-1] + (groups, shape_in[-1] // groups)
    left_real = first_pair[0].reshape(split_shape)
    left_imag = first_pair[1].reshape(split_shape)
    right_real = second_pair[0].reshape(split_shape)
    right_imag = second_pair[1].reshape(split_shape)
    out_real = jnp.sum(left_real * right_real + left_imag * right_imag, axis=-1)
    out_imag = jnp.sum(left_real * right_imag - left_imag * right_real, axis=-1)
    return (out_real, out_imag)


def project(pooled_in, target, weights, w_cols):
    gathered = lax.all_gather(pooled_in, "chan", axis=1, tiled=True)
    output = jnp.dot(gathered, w_cols, preferred_element_type=jnp.float32)
    deviation = (weights[:, None] * (output - target.astype(jnp.float32))).astype(jnp.bfloat16)
    partial_w = lax.dot_general(
        gathered, deviation, (((0,), (0,)), ((), ())), preferred_element_type=jnp.float32
    )
    weight_grad = lax.psum_scatter(partial_w, "seq", scatter_dimension=0, tiled=True)
    channel_back = lax.psum_scatter(
        lax.dot_general(
            w_cols, deviation, (((1,), (1,)), ((), ())), preferred_element_type=jnp.float32
        ),
        "chan",
        scatter_dimension=0,
        tiled=True,
    )
    back_outer = channel_back.T
    return (back_outer, weight_grad)


def per_device(
    values,
    gate_inner,
    gate_outer,
    filter_one,
    filter_two,
    teacher,
    w_out,
    gene_ids,
    cell_lengths,
    gene_weights,
):
    shard_count = lax.axis_size("seq")
    position = lax.axis_index("seq")
    length = values.shape[0]
    channels = values.shape[1]
    groups = filter_one.shape[0]
    tables = make_tables(length, shard_count, position)
    token_pos = position * length + jnp.arange(length, dtype=jnp.int32)
    starts = jnp.cumsum(cell_lengths) - cell_lengths
    opening = jnp.any(token_pos[:, None] == starts[None, :], axis=1)
    weights = jnp.take(gene_weights, gene_ids, axis=0) * jnp.where(opening, 0.0, 1.0)
    stacked = jnp.concatenate([values.astype(jnp.float32), filter_one.T, filter_two.T], axis=1)
    spectra = spectrum(stacked, tables)
    spec_values = take_range(spectra, 0, channels)
    spec_one = take_range(spectra, channels, channels + groups)
    spec_two = take_range(spectra, channels + groups, channels + 2 * groups)
    first_conv = signal_rows(filtered(spec_values, spec_one, False), tables)
    spec_inner = spectrum(gate_inner * first_conv, tables)
    second_conv = signal_rows(filtered(spec_inner, spec_two, False), tables)
    pooled_in = (gate_outer * second_conv).astype(jnp.bfloat16)
    back_outer, grad_w_out = project(pooled_in, teacher, weights, w_out)
    grad_outer = (back_outer * second_conv).astype(jnp.bfloat16)
    spec_second = spectrum(back_outer * gate_outer, tables)
    merged = signal_rows(
        joined(filtered(spec_second, spec_two, True), pooled(spec_inner, spec_second, groups)),
        tables,
    )
    back_inner = merged[:, :channels]
    grad_two = merged[:, channels:]
    grad_inner = (back_inner * first_conv).astype(jnp.bfloat16)
    spec_first = spectrum(back_inner * gate_inner, tables)
    merged = signal_rows(
        joined(filtered(spec_first, spec_one, True), pooled(spec_values, spec_first, groups)),
        tables,
    )
    grad_values = merged[:, :channels].astype(jnp.bfloat16)
    grad_one = merged[:, channels:]
    return (grad_values, grad_inner, grad_outer, grad_one.T, grad_two.T, grad_w_out)


def solution(mesh):
    return jax.shard_map(
        per_device,
        mesh=mesh,
        in_specs=(
            P("seq", "chan"),
            P("seq", "chan"),
            P("seq", "chan"),
            P("chan", "seq"),
            P("chan", "seq"),
            P("seq", "chan"),
            P(None, "chan"),
            P("seq"),
            P(),
            P(),
        ),
        out_specs=(
            P("seq", "chan"),
            P("seq", "chan"),
            P("seq", "chan"),
            P("chan", "seq"),
            P("chan", "seq"),
            P("seq", "chan"),
        ),
        check_vma=False,
    )
```

profile of v0, /device:TPU:1, one launch (start us, length us, event | category | flops | bytes accessed | tf_op | source)
XLA Modules:
  0.0 554.5 jit_solution(16846920802349217116)
XLA Ops:
  8.0 0.8 convert_element_type.117
  9.5 0.7 copy.332
  10.2 17.2 %all-to-all-start = ((f32[128,1,66]{2,1,0:T(1,128)}), f32[128,1,66]{2,1,0:T(1,128)S(1)}, u32[]{:S(2)}, u32[]{:S(2)}) async-start(f32[128,1,66]{2,1,0:T(1,128)} %copy.332), calls=%async_computation | async-start | bytes 131072 | tf_op jit(solution)/shard_map/all_to_all | solution.py:33
  27.6 11.7 %all-to-all-done = f32[128,1,66]{2,1,0:T(1,128)S(1)} async-done(((f32[128,1,66]{2,1,0:T(1,128)}), f32[128,1,66]{2,1,0:T(1,128)S(1)}, u32[]{:S(2)}, u32[]{:S(2)}) %all-to-all-start) | async-done | bytes 33824 | tf_op jit(solution)/shard_map/all_to_all | solution.py:33
  40.2 0.9 copy.334
  41.1 4.4 all-to-all-start.1
  45.7 13.3 %all-to-all-done.1 = f32[4,64,132]{2,0,1:T(4,128)S(1)} async-done(((f32[4,64,132]{2,0,1:T(4,128)}), f32[4,64,132]{2,0,1:T(4,128)S(1)}, u32[]{:S(2)}, u32[]{:S(2)}) %all-to-all-start.1) | async-done | bytes 135200 | tf_op jit(solution)/shard_map/all_to_all | solution.py:37
  62.4 18.2 %all_to_all.276 = f32[128,2,128]{2,1,0:T(2,128)S(1)} all-to-all(f32[128,2,128]{2,1,0:T(2,128)S(1)} %copy.341), channel_id=1, replica_groups=mesh['seq'=32,'chan'=16] {'seq'}, dimensions={0} | all-to-all | bytes 262144 | tf_op jit(solution)/shard_map/all_to_all | solution.py:33
  81.4 0.7 reshape.508
  82.1 4.8 all-to-all-start.3
  87.0 11.9 %all-to-all-done.3 = f32[32,1,256]{2,1,0:T(1,128)S(1)} async-done(((f32[32,1,256]{2,1,0:T(1,128)}), f32[32,1,256]{2,1,0:T(1,128)S(1)}, u32[]{:S(2)}, u32[]{:S(2)}) %all-to-all-start.3) | async-done | bytes 32800 | tf_op jit(solution)/shard_map/all_to_all | solution.py:37
  100.2 0.8 reduce.13
  101.2 15.4 %all_to_all.277 = f32[32,1,256]{2,1,0:T(1,128)S(1)} all-to-all(f32[32,1,256]{2,1,0:T(1,128)S(1)} %reshape.510), channel_id=1, replica_groups=mesh['seq'=32,'chan'=16] {'seq'}, dimensions={0} | all-to-all | bytes 65536 | tf_op jit(solution)/shard_map/all_to_all | solution.py:33
  118.3 0.7 copy.347
  119.0 4.4 all-to-all-start.5
  124.6 11.2 %all-to-all-done.5 = f32[4,64,128]{2,0,1:T(4,128)S(1)} async-done(((f32[4,64,128]{2,0,1:T(4,128)}), f32[4,64,128]{2,0,1:T(4,128)S(1)}, u32[]{:S(2)}, u32[]{:S(2)}) %all-to-all-start.5) | async-done | bytes 131104 | tf_op jit(solution)/shard_map/all_to_all | solution.py:37
  138.5 0.7 copy.357
  139.2 4.9 all-to-all-start.6
  144.1 1.1 gather_fusion
  145.4 10.9 %all-to-all-done.6 = f32[128,2,128]{2,1,0:T(2,128)S(1)} async-done(((f32[128,2,128]{2,1,0:T(2,128)}), f32[128,2,128]{2,1,0:T(2,128)S(1)}, u32[]{:S(2)}, u32[]{:S(2)}) %all-to-all-start.6) | async-done | bytes 131104 | tf_op jit(solution)/shard_map/all_to_all | solution.py:33
  157.1 0.7 reshape.512
  157.8 4.8 all-to-all-start.7
  162.8 11.7 %all-to-all-done.7 = f32[32,1,256]{2,1,0:T(1,128)S(1)} async-done(((f32[32,1,256]{2,1,0:T(1,128)}), f32[32,1,256]{2,1,0:T(1,128)S(1)}, u32[]{:S(2)}, u32[]{:S(2)}) %all-to-all-start.7) | async-done | bytes 32800 | tf_op jit(solution)/shard_map/all_to_all | solution.py:37
  175.5 34.6 %all_gather.3 = bf16[128,1024]{0,1:T(8,128)(2,1)S(1)} all-gather(bf16[128,64]{0,1:T(8,128)(2,1)S(1)} %copy.361), channel_id=1, replica_groups=mesh['seq'=32,'chan'=16] {'chan'}, dimensions={1}, use_global_device_ids=true | all-gather | bytes 278528 | tf_op jit(solution)/shard_map/all_gather | solution.py:142
  210.5 1.0 copy.391
  211.6 72.6 %reduce-scatter.7.cloned.1.call-done = f32[64,128]{1,0:T(8,128)} async-done(((f32[1024,128]{1,0:T(8,128)}), f32[64,128]{1,0:T(8,128)}) %reduce-scatter.7.cloned.1.call-update) | async-done | bytes 32784
  284.1 0.8 copy.392
  285.0 0.8 reduce.16
  285.9 32.8 %all_to_all.278 = f32[32,1,256]{2,1,0:T(1,128)S(1)} all-to-all(f32[32,1,256]{2,1,0:T(1,128)S(1)} %reshape.514), channel_id=1, replica_groups=mesh['seq'=32,'chan'=16] {'seq'}, dimensions={0} | all-to-all | bytes 65536 | tf_op jit(solution)/shard_map/all_to_all | solution.py:33
  318.8 0.7 reduce.17
  320.5 0.7 copy.364
  321.3 4.3 all-to-all-start.9
  325.6 12.2 %all-to-all-done.9 = f32[4,64,128]{2,0,1:T(4,128)S(1)} async-done(((f32[4,64,128]{2,0,1:T(4,128)}), f32[4,64,128]{2,0,1:T(4,128)S(1)}, u32[]{:S(2)}, u32[]{:S(2)}) %all-to-all-start.9) | async-done | bytes 131104 | tf_op jit(solution)/shard_map/all_to_all | solution.py:37
  341.3 17.6 %all_to_all.279 = f32[128,2,130]{2,1,0:T(2,128)S(1)} all-to-all(f32[128,2,130]{2,1,0:T(2,128)S(1)} %copy.374), channel_id=1, replica_groups=mesh['seq'=32,'chan'=16] {'seq'}, dimensions={0} | all-to-all | bytes 266240 | tf_op jit(solution)/shard_map/all_to_all | solution.py:33
  359.8 18.0 %all_to_all.280 = f32[4,32,65]{2,0,1:T(4,128)S(1)} all-to-all(f32[4,32,65]{2,0,1:T(4,128)S(1)} %copy.376), channel_id=1, replica_groups=mesh['seq'=32,'chan'=16] {'seq'}, dimensions={1} | all-to-all | bytes 66560 | tf_op jit(solution)/shard_map/all_to_all | solution.py:37
  377.8 0.8 reduce.18
  378.7 15.4 %all_to_all.281 = f32[32,1,256]{2,1,0:T(1,128)S(1)} all-to-all(f32[32,1,256]{2,1,0:T(1,128)S(1)} %reshape.516), channel_id=1, replica_groups=mesh['seq'=32,'chan'=16] {'seq'}, dimensions={0} | all-to-all | bytes 65536 | tf_op jit(solution)/shard_map/all_to_all | solution.py:33
  394.1 0.7 reduce.19
  395.9 0.7 copy.379
  396.6 4.3 all-to-all-start.13
  400.9 12.2 %all-to-all-done.13 = f32[4,64,128]{2,0,1:T(4,128)S(1)} async-done(((f32[4,64,128]{2,0,1:T(4,128)}), f32[4,64,128]{2,0,1:T(4,128)S(1)}, u32[]{:S(2)}, u32[]{:S(2)}) %all-to-all-start.13) | async-done | bytes 131104 | tf_op jit(solution)/shard_map/all_to_all | solution.py:37
  416.2 0.8 copy.385
  417.0 4.7 all-to-all-start.14
  421.8 1.0 fusion.357
  424.2 10.9 %all-to-all-done.14 = f32[128,2,130]{2,1,0:T(2,128)S(1)} async-done(((f32[128,2,130]{2,1,0:T(2,128)}), f32[128,2,130]{2,1,0:T(2,128)S(1)}, u32[]{:S(2)}, u32[]{:S(2)}) %all-to-all-start.14) | async-done | bytes 133152 | tf_op jit(solution)/shard_map/all_to_all | solution.py:33
  436.6 6.3 %all-to-all-start.15 = ((f32[4,32,65]{2,0,1:T(4,128)}), f32[4,32,65]{2,0,1:T(4,128)S(1)}, u32[]{:S(2)}, u32[]{:S(2)}) async-start(f32[4,32,65]{2,0,1:T(4,128)} %copy.387), calls=%async_computation.15 | async-start | bytes 131072 | tf_op jit(solution)/shard_map/all_to_all | solution.py:37
  443.6 11.1 %all-to-all-done.15 = f32[4,32,65]{2,0,1:T(4,128)S(1)} async-done(((f32[4,32,65]{2,0,1:T(4,128)}), f32[4,32,65]{2,0,1:T(4,128)S(1)}, u32[]{:S(2)}, u32[]{:S(2)}) %all-to-all-start.15) | async-done | bytes 33312 | tf_op jit(solution)/shard_map/all_to_all | solution.py:37
  456.1 91.0 %reduce-scatter.5.cloned.1.call-done = f32[32,64]{1,0:T(8,128)} async-done(((f32[1024,64]{1,0:T(8,128)}), f32[32,64]{1,0:T(8,128)}) %reduce-scatter.5.cloned.1.call-update) | async-done | bytes 8208 | tf_op jit(solution)/shard_map/reduce_scatter | solution.py:148
  (184 shorter events, 29.6 us)
Async XLA Ops:
  8.0 202.1 %copy-start = (bf16[1024,64]{0,1:T(8,128)(2,1)S(1)}, bf16[1024,64]{0,1:T(8,128)(2,1)}, u32[]{:S(2)}) copy-start(bf16[1024,64]{0,1:T(8,128)(2,1)} %param.16) | copy-start | bytes 393220
  8.8 0.7 copy-start.5
  8.8 0.7 copy-start.6
  10.2 29.1 %all-to-all-start = ((f32[128,1,66]{2,1,0:T(1,128)}), f32[128,1,66]{2,1,0:T(1,128)S(1)}, u32[]{:S(2)}, u32[]{:S(2)}) async-start(f32[128,1,66]{2,1,0:T(1,128)} %copy.332), calls=%async_computation | async-start | bytes 131072 | tf_op jit(solution)/shard_map/all_to_all | solution.py:33
  41.1 17.9 %all-to-all-start.1 = ((f32[4,64,132]{2,0,1:T(4,128)}), f32[4,64,132]{2,0,1:T(4,128)S(1)}, u32[]{:S(2)}, u32[]{:S(2)}) async-start(f32[4,64,132]{2,0,1:T(4,128)} %copy.334), calls=%async_computation.1 | async-start | bytes 524288 | tf_op jit(solution)/shard_map/all_to_all | solution.py:37
  82.1 4.8 copy-start.2
  82.1 16.8 %all-to-all-start.3 = ((f32[32,1,256]{2,1,0:T(1,128)}), f32[32,1,256]{2,1,0:T(1,128)S(1)}, u32[]{:S(2)}, u32[]{:S(2)}) async-start(f32[32,1,256]{2,1,0:T(1,128)} %reshape.508), calls=%async_computation.3 | async-start | bytes 65536 | tf_op jit(solution)/shard_map/all_to_all | solution.py:37
  119.0 4.4 copy-start.7
  119.0 16.7 %all-to-all-start.5 = ((f32[4,64,128]{2,0,1:T(4,128)}), f32[4,64,128]{2,0,1:T(4,128)S(1)}, u32[]{:S(2)}, u32[]{:S(2)}) async-start(f32[4,64,128]{2,0,1:T(4,128)} %copy.347), calls=%async_computation.5 | async-start | bytes 262144 | tf_op jit(solution)/shard_map/all_to_all | solution.py:37
  123.5 0.7 copy-start.8
  139.2 4.9 copy-start.1
  139.2 17.1 %all-to-all-start.6 = ((f32[128,2,128]{2,1,0:T(2,128)}), f32[128,2,128]{2,1,0:T(2,128)S(1)}, u32[]{:S(2)}, u32[]{:S(2)}) async-start(f32[128,2,128]{2,1,0:T(2,128)} %copy.357), calls=%async_computation.6 | async-start | bytes 262144 | tf_op jit(solution)/shard_map/all_to_all | solution.py:33
  157.8 4.9 copy-start.3
  157.8 16.7 %all-to-all-start.7 = ((f32[32,1,256]{2,1,0:T(1,128)}), f32[32,1,256]{2,1,0:T(1,128)S(1)}, u32[]{:S(2)}, u32[]{:S(2)}) async-start(f32[32,1,256]{2,1,0:T(1,128)} %reshape.512), calls=%async_computation.7 | async-start | bytes 65536 | tf_op jit(solution)/shard_map/all_to_all | solution.py:37
  162.6 121.5 %reduce-scatter.7.cloned.1.call-start = ((), (), s32[]{:S(2)}) async-start(), calls=%async_computation.19 | async-start | bytes 557056
  175.5 34.6 %copy-start.4 = (bf16[128,64]{0,1:T(8,128)(2,1)S(1)}, bf16[128,64]{0,1:T(8,128)(2,1)}, u32[]{:S(2)}) copy-start(bf16[128,64]{0,1:T(8,128)(2,1)} %param.15) | copy-start | bytes 49156
  321.3 16.5 %all-to-all-start.9 = ((f32[4,64,128]{2,0,1:T(4,128)}), f32[4,64,128]{2,0,1:T(4,128)S(1)}, u32[]{:S(2)}, u32[]{:S(2)}) async-start(f32[4,64,128]{2,0,1:T(4,128)} %copy.364), calls=%async_computation.9 | async-start | bytes 262144 | tf_op jit(solution)/shard_map/all_to_all | solution.py:37
  396.6 16.5 %all-to-all-start.13 = ((f32[4,64,128]{2,0,1:T(4,128)}), f32[4,64,128]{2,0,1:T(4,128)S(1)}, u32[]{:S(2)}, u32[]{:S(2)}) async-start(f32[4,64,128]{2,0,1:T(4,128)} %copy.379), calls=%async_computation.13 | async-start | bytes 262144 | tf_op jit(solution)/shard_map/all_to_all | solution.py:37
  417.0 18.1 %all-to-all-start.14 = ((f32[128,2,130]{2,1,0:T(2,128)}), f32[128,2,130]{2,1,0:T(2,128)S(1)}, u32[]{:S(2)}, u32[]{:S(2)}) async-start(f32[128,2,130]{2,1,0:T(2,128)} %copy.385), calls=%async_computation.14 | async-start | bytes 524288 | tf_op jit(solution)/shard_map/all_to_all | solution.py:33
  421.8 125.3 %reduce-scatter.5.cloned.1.call-start = ((), (), s32[]{:S(2)}) async-start(), calls=%async_computation.18 | async-start | bytes 540672 | tf_op jit(solution)/shard_map/reduce_scatter | solution.py:148
  436.6 18.1 %all-to-all-start.15 = ((f32[4,32,65]{2,0,1:T(4,128)}), f32[4,32,65]{2,0,1:T(4,128)S(1)}, u32[]{:S(2)}, u32[]{:S(2)}) async-start(f32[4,32,65]{2,0,1:T(4,128)} %copy.387), calls=%async_computation.15 | async-start | bytes 131072 | tf_op jit(solution)/shard_map/all_to_all | solution.py:37
Sparse Core Ops, SparseCore 0:
  211.7 72.4 reduce-scatter.6
Sparse Core Ops, SparseCore 1:
  428.1 119.0 reduce-scatter.4
where the time goes:
time: 560 us; the launch traced here: 555 us
  waiting for transfers between devices  281 us (50%)
  blocking collectives  152 us (27%)
  starting transfers between devices  60.3 us (11%)
  local copies, waits for them, and re-layouts  20.5 us (4%)
  between operations  16.6 us (3%)
  matrix products  16.1 us (3%)
  other arithmetic  8.36 us (1%)
    all_to_all x5, blocking collectives, spread_out(): lax.all_to_all(packed, 'seq', split_axis=0, concat_axis=1, tiled=True)  99.4 us
    reduce_scatter x1, waiting for transfers between devices, project(): lax.psum_scatter(partial_w, 'seq', scatter_dimension=0, tiled=True)  91 us
    all_to_all x7, waiting for transfers between devices, bring_back(): lax.all_to_all(packed, 'seq', split_axis=1, concat_axis=0, tiled=True)  83.6 us
    unnamed x3, waiting for transfers between devices  72.6 us
    all_gather x1, blocking collectives, project(): gathered = lax.all_gather(pooled_in, 'chan', axis=1, tiled=True)  34.6 us
    all_to_all x3, waiting for transfers between devices, spread_out(): lax.all_to_all(packed, 'seq', split_axis=0, concat_axis=1, tiled=True)  33.5 us
    all_to_all x7, starting transfers between devices, bring_back(): lax.all_to_all(packed, 'seq', split_axis=1, concat_axis=0, tiled=True)  33.4 us
    all_to_all x3, starting transfers between devices, spread_out(): lax.all_to_all(packed, 'seq', split_axis=0, concat_axis=1, tiled=True)  26.9 us
  transfers between devices with their start and end apart: 12, of which 12 were waited for; matrix products, arithmetic and copies ran while one was open for 1% of the time, Pallas kernels for 0%

commit v1 on v0

v1 whole, which is shorter than its diff:
```python
import functools

import jax
import jax.numpy as jnp
from jax import lax
from jax.experimental import pallas as pl
from jax.experimental.pallas import tpu as pltpu
from jax.sharding import PartitionSpec as P

F32 = jnp.float32
BF16 = jnp.bfloat16
MESH = pl.DeviceIdType.MESH
HIGHEST = lax.Precision.HIGHEST
LANES = 128


def nn(left, right, precision=None):
    return lax.dot_general(
        left, right, (((1,), (0,)), ((), ())), precision=precision, preferred_element_type=F32
    )


def nt(left, right):
    return lax.dot_general(left, right, (((1,), (1,)), ((), ())), preferred_element_type=F32)


def tn(left, right, precision=None):
    return lax.dot_general(
        left, right, (((0,), (0,)), ((), ())), precision=precision, preferred_element_type=F32
    )


def split(value):
    high = value.astype(BF16)
    return high, (value - high.astype(F32)).astype(BF16)


def multiple(index, factor):
    return pl.multiple_of(index * factor, factor)


def kernel(
    blocks,
    groups,
    values,
    gate_inner,
    gate_outer,
    teacher,
    filter_one,
    filter_two,
    w_out,
    gene_ids,
    cell_lengths,
    table,
    out_values,
    out_inner,
    out_outer,
    out_one,
    out_two,
    out_w,
    stage,
    send1,
    recv1,
    flat1,
    pad_one,
    pad_two,
    gate_c,
    conv_c,
    lags_one,
    lags_two,
    big_one,
    big_two,
    toe_one,
    toe_two,
    strip_one,
    strip_two,
    send2,
    recv2,
    second_t,
    outer_t,
    teach_t,
    w_blocks,
    w_rows,
    token_w,
    pooled_t,
    pooled_all,
    dev_t,
    dev_all,
    gw_send,
    gw_recv,
    send5,
    recv5,
    flat5,
    big_back,
    cross,
    sums,
    flat6,
    send6,
    recv6,
    send_sem,
    recv_sem,
):
    half_count = blocks // 2
    channels = values.shape[0]
    share = channels // half_count
    rows = share * blocks
    own_rows = share * half_count
    row1 = send1.shape[1]
    row6 = send6.shape[1]
    s = lax.axis_index("seq")
    g = lax.axis_index("chan")
    half = lax.div(s, half_count)
    place = lax.rem(s, half_count)

    barrier = pltpu.get_barrier_semaphore()

    def greet_seq(step, carry):
        pl.semaphore_signal(
            barrier, inc=1, device_id={"seq": lax.rem(s + step, blocks)}, device_id_type=MESH
        )
        return carry

    def greet_chan(step, carry):
        pl.semaphore_signal(
            barrier, inc=1, device_id={"chan": lax.rem(g + step, groups)}, device_id_type=MESH
        )
        return carry

    lax.fori_loop(1, blocks, greet_seq, 0)
    lax.fori_loop(1, groups, greet_chan, 0)

    def remote(src, dst, index, device):
        return pltpu.make_async_remote_copy(
            src_ref=src,
            dst_ref=dst,
            send_sem=send_sem.at[index],
            recv_sem=recv_sem.at[index],
            device_id=device,
            device_id_type=MESH,
        )

    def to_seq(index, src_of, dst):
        def body(step, carry):
            peer = lax.rem(s + step, blocks)
            remote(src_of(peer), dst, index, {"seq": peer}).start()
            return carry

        lax.fori_loop(1, blocks, body, 0)
        pltpu.make_async_copy(src_of(s), dst, recv_sem.at[index]).start()

    def to_half(index, src_of, dst):
        def body(step, carry):
            peer = lax.rem(place + step, half_count)
            remote(src_of(peer), dst, index, {"seq": half * half_count + peer}).start()
            return carry

        lax.fori_loop(1, half_count, body, 0)
        pltpu.make_async_copy(src_of(place), dst, recv_sem.at[index]).start()

    def to_chan(index, src_of, dst):
        def body(step, carry):
            peer = lax.rem(g + step, groups)
            remote(src_of(peer), dst, index, {"chan": peer}).start()
            return carry

        lax.fori_loop(1, groups, body, 0)
        pltpu.make_async_copy(src_of(g), dst, recv_sem.at[index]).start()

    def arrived(index, ref):
        pltpu.make_async_copy(ref, ref, recv_sem.at[index]).wait()

    def sent(index, ref):
        pltpu.make_async_copy(ref, ref, send_sem.at[index]).wait()

    values_t = values[...].astype(F32)
    inner_t = gate_inner[...].astype(F32)
    high_one, low_one = split(filter_one[...])
    high_two, low_two = split(filter_two[...])
    filter_rows = jnp.concatenate(
        [high_one.astype(F32), low_one.astype(F32), high_two.astype(F32), low_two.astype(F32)], axis=0
    )
    for p in range(half_count):
        stage[p, 0:share, :] = values_t[p * share : (p + 1) * share]
        stage[p, share : 2 * share, :] = inner_t[p * share : (p + 1) * share]
        stage[p, 2 * share : 2 * share + 4, :] = filter_rows
        if 2 * share + 4 < row1:
            stage[p, 2 * share + 4 : row1, :] = jnp.zeros((row1 - 2 * share - 4, LANES), F32)
    send1[...] = stage[...].astype(BF16)
    pl.semaphore_wait(barrier, blocks + groups - 2)
    to_seq(0, lambda peer: send1.at[lax.rem(peer, half_count)], recv1.at[s])
    to_chan(
        1,
        lambda peer: w_out.at[:, pl.ds(multiple(lax.div(peer, 2), LANES), LANES)],
        w_blocks.at[g],
    )

    outer_t[...] = gate_outer[...].astype(F32)
    teach_t[...] = teacher[...].astype(F32)
    ids = gene_ids[...]
    hot_rows = (
        lax.broadcasted_iota(jnp.int32, (table.shape[0], LANES), 0) == lax.shift_right_logical(ids, 7)
    ).astype(F32)
    picked = tn(table[...], hot_rows, HIGHEST)
    hot_lanes = lax.broadcasted_iota(jnp.int32, (LANES, LANES), 0) == jnp.bitwise_and(ids, 127)
    weight = jnp.sum(jnp.where(hot_lanes, picked, 0.0), axis=0, keepdims=True)
    token = s * LANES + lax.broadcasted_iota(jnp.int32, (1, LANES), 1)
    opening = token == 0
    start = cell_lengths[0]
    for cell in range(1, cell_lengths.shape[0]):
        opening = jnp.logical_or(opening, token == start)
        start = start + cell_lengths[cell]
    token_w[...] = jnp.where(opening, 0.0, weight)

    row_iota = lax.broadcasted_iota(jnp.int32, (LANES, LANES), 0)
    lane_iota = lax.broadcasted_iota(jnp.int32, (LANES, LANES), 1)
    keep = lane_iota >= row_iota
    flip = (row_iota + lane_iota == LANES - 1).astype(BF16)

    arrived(0, recv1)
    flat1[...] = recv1[...].astype(F32).reshape(blocks * row1, LANES)

    def every(ref, first, stride):
        return ref[pl.ds(first, blocks, stride=stride), :]

    zeros = jnp.zeros((blocks, LANES), F32)
    for c in range(share):
        pad_one[c, 0:blocks, :] = zeros
        pad_one[c, blocks : 2 * blocks, :] = every(flat1, c, row1)
        pad_two[c, 0:blocks, :] = zeros
        gate_c[c * blocks : (c + 1) * blocks, :] = every(flat1, share + c, row1)
    lags_one[...] = every(flat1, 2 * share, row1) + every(flat1, 2 * share + 1, row1)
    lags_two[...] = every(flat1, 2 * share + 2, row1) + every(flat1, 2 * share + 3, row1)

    def toeplitz(lags, toe):
        def body(m, before):
            row = lags[pl.ds(m, 1), :]
            turned = pltpu.roll(
                jnp.broadcast_to(row, (LANES, LANES)), 0, axis=1, stride=1, stride_axis=0
            )
            high, low = split(jnp.where(keep, turned, before))
            at = pl.ds(multiple(m, LANES), LANES)
            toe[at, 0:LANES] = high
            toe[at, LANES : 2 * LANES] = low
            return turned

        lax.fori_loop(0, blocks, body, jnp.zeros((LANES, LANES), F32))

    def stripe(toe, strip):
        def body(m, carry):
            at = pl.ds(multiple(m, LANES), LANES)
            strip[0:LANES, at] = toe[at, 0:LANES]
            strip[LANES : 2 * LANES, at] = toe[at, LANES : 2 * LANES]
            return carry

        lax.fori_loop(0, blocks, body, 0)

    def spread(pad, big, backward):
        for m in range(blocks):
            first = m if backward else blocks - m
            for c in range(share):
                big[c * blocks : (c + 1) * blocks, m * LANES : (m + 1) * LANES] = pad[
                    c, first : first + blocks, :
                ].astype(BF16)

    length = blocks * LANES

    def own(read):
        return jnp.concatenate(
            [
                read(pl.ds(pl.multiple_of(c * blocks + half * half_count, half_count), half_count))
                for c in range(share)
            ],
            axis=0,
        )

    def joined(product):
        return product[:, 0:LANES] + product[:, LANES : 2 * LANES]

    spread(pad_one, big_one, False)
    toeplitz(lags_one, toe_one)
    first_conv = joined(nn(big_one[:, 0:length], toe_one[...]))
    conv_c[...] = first_conv
    inner_prod = gate_c[...] * first_conv
    for c in range(share):
        pad_two[c, blocks : 2 * blocks, :] = inner_prod[c * blocks : (c + 1) * blocks]
    spread(pad_two, big_two, False)
    toeplitz(lags_two, toe_two)
    second = joined(nn(own(lambda at: big_two[at, 0:length]), toe_two[...]))
    row2 = send2.shape[0] // half_count
    for c in range(share):
        send2[pl.ds(c, half_count, stride=row2), :] = second[c * half_count : (c + 1) * half_count]
    to_half(
        2,
        lambda peer: send2.at[pl.ds(multiple(peer, row2), row2), :],
        recv2.at[pl.ds(multiple(place, row2), row2), :],
    )
    stripe(toe_two, strip_two)
    stripe(toe_one, strip_one)
    arrived(1, w_blocks)
    stacked = w_blocks[...].astype(F32).reshape(groups * channels, LANES)
    w_rows[...] = stacked.T.astype(BF16)

    arrived(2, recv2)
    for p in range(half_count):
        second_t[p * share : (p + 1) * share, :] = recv2[p * row2 : p * row2 + share, :]
    pooled_t[...] = (outer_t[...] * second_t[...]).astype(BF16)
    to_chan(3, lambda peer: pooled_t, pooled_all.at[g])
    arrived(3, pooled_all)
    width = groups * channels
    pooled = pooled_all[...].reshape(width, LANES)
    output = nn(w_out[...], pooled)
    deviation = (token_w[...] * (output - teach_t[...])).astype(BF16)
    dev_t[...] = deviation
    to_chan(4, lambda peer: dev_t, dev_all.at[g])

    share_w = width // blocks
    part = share_w // 2
    parts = pooled.reshape(blocks, 2, part, LANES)
    left = jnp.concatenate(
        [parts[:, 0].reshape(blocks * part, LANES), parts[:, 1].reshape(blocks * part, LANES)], axis=1
    )
    empty = jnp.zeros_like(deviation)
    right = jnp.concatenate(
        [jnp.concatenate([deviation, empty], axis=1), jnp.concatenate([empty, deviation], axis=1)], axis=0
    )
    gw_send[...] = nt(left, right).reshape(blocks, part, LANES).astype(gw_send.dtype)
    to_seq(5, lambda peer: gw_send.at[peer], gw_recv.at[s])

    arrived(4, dev_all)
    back_outer = nn(w_rows[pl.ds(multiple(lax.rem(g, 2), channels), channels), :], dev_all[...].reshape(width, LANES))
    back_second = back_outer * outer_t[...]
    send5[...] = back_second.astype(BF16).reshape(half_count, share, LANES)
    to_seq(6, lambda peer: send5.at[lax.rem(peer, half_count)], recv5.at[s])
    out_outer[...] = (back_outer * second_t[...]).astype(BF16)

    arrived(6, recv5)
    flat5[...] = recv5[...].astype(F32).reshape(rows, LANES)
    signal = [every(flat5, c, share) for c in range(share)]
    for c in range(share):
        pad_two[c, 0:blocks, :] = signal[c]
        pad_two[c, blocks : 2 * blocks, :] = zeros
    spread(pad_two, big_back, True)
    back_inner = joined(nt(big_back[...], strip_two[...]))
    back_first = back_inner * gate_c[...]
    for c in range(share):
        pad_one[c, 0:blocks, :] = back_first[c * blocks : (c + 1) * blocks]
        pad_one[c, blocks : 2 * blocks, :] = zeros
    grad_inner_c = back_inner * conv_c[...]
    conv_c[...] = grad_inner_c

    def filter_grad(back, big, column):
        turned = nt(flip, back.astype(BF16)).astype(BF16)
        window = big[:, pl.ds(multiple(half, half_count * LANES), (half_count + 1) * LANES)]
        cross[...] = nn(turned, window)

        def rolled(m):
            at = pl.ds(multiple(m, LANES), LANES)
            return pltpu.roll(cross[:, at], 0, axis=1, stride=1, stride_axis=0)

        def body(m, current):
            later = rolled(m + 1)
            sums[pl.ds(m, 1), :] = jnp.sum(jnp.where(keep, current, later), axis=0, keepdims=True)
            return later

        lax.fori_loop(0, half_count, body, rolled(0))
        high, low = split(sums[...])
        flat6[pl.ds(column, half_count, stride=row6), :] = high.astype(F32)
        flat6[pl.ds(column + 1, half_count, stride=row6), :] = low.astype(F32)

    for big in (big_one, big_two):
        big[:, length : length + LANES] = jnp.zeros((rows, LANES), BF16)
    filter_grad(jnp.concatenate(signal, axis=0), big_two, 2 * share + 2)
    filter_grad(back_first, big_one, 2 * share)
    spread(pad_one, big_back, True)
    grad_values_c = joined(nt(own(lambda at: big_back[at, :]), strip_one[...]))
    grad_inner_own = own(lambda at: conv_c[at, :])
    for c in range(share):
        at = slice(c * half_count, (c + 1) * half_count)
        flat6[pl.ds(c, half_count, stride=row6), :] = grad_values_c[at]
        flat6[pl.ds(share + c, half_count, stride=row6), :] = grad_inner_own[at]
    for c in range(2 * share + 4, row6):
        flat6[pl.ds(c, half_count, stride=row6), :] = jnp.zeros((half_count, LANES), F32)
    send6[...] = flat6[...].reshape(half_count, row6, LANES).astype(BF16)
    to_half(7, lambda peer: send6.at[peer], recv6.at[place])

    arrived(5, gw_recv)
    total_w = jnp.sum(gw_recv[...].astype(F32), axis=0)
    out_w[0:part, :] = total_w[:, 0:channels]
    out_w[part:share_w, :] = total_w[:, channels : 2 * channels]

    arrived(7, recv6)
    flat6[...] = recv6[...].astype(F32).reshape(half_count * row6, LANES)
    for p in range(half_count):
        second_t[p * share : (p + 1) * share, :] = flat6[p * row6 : p * row6 + share, :]
        outer_t[p * share : (p + 1) * share, :] = flat6[p * row6 + share : p * row6 + 2 * share, :]
    out_values[...] = second_t[...].astype(BF16)
    out_inner[...] = outer_t[...].astype(BF16)
    lag_rows = []
    for column in (2 * share, 2 * share + 2):
        both = flat6[pl.ds(column, half_count, stride=row6), :] + flat6[
            pl.ds(column + 1, half_count, stride=row6), :
        ]
        lag_rows.append(jnp.sum(both, axis=0, keepdims=True))
    lag_rows.append(jnp.zeros((6, LANES), F32))
    ordered = nn(jnp.concatenate(lag_rows, axis=0), flip.astype(F32), HIGHEST)
    out_one[...] = ordered[0:1]
    out_two[...] = ordered[1:2]

    sent(0, recv1.at[pl.ds(0, blocks - 1)])
    sent(1, w_blocks.at[pl.ds(0, groups - 1)])
    sent(2, recv2.at[pl.ds(0, row2 * (half_count - 1)), :])
    sent(3, pooled_all.at[pl.ds(0, groups - 1)])
    sent(4, dev_all.at[pl.ds(0, groups - 1)])
    sent(5, gw_recv.at[pl.ds(0, blocks - 1)])
    sent(6, recv5.at[pl.ds(0, blocks - 1)])
    sent(7, recv6.at[pl.ds(0, half_count - 1)])


def rounded(count, factor):
    return -(-count // factor) * factor


def per_device(
    blocks,
    groups,
    values,
    gate_inner,
    gate_outer,
    filter_one,
    filter_two,
    teacher,
    w_out,
    gene_ids,
    cell_lengths,
    gene_weights,
):
    length, channels = values.shape
    half_count = blocks // 2
    share = channels // half_count
    rows = share * blocks
    width = groups * channels
    share_w = width // blocks
    row1 = rounded(2 * share + 4, 16)
    row2 = rounded(share, 8)
    span = blocks * LANES
    vocab = gene_weights.shape[0]
    padded = rounded(vocab, 8 * LANES)
    table = jnp.pad(gene_weights, (0, padded - vocab)).reshape(padded // LANES, LANES)
    vmem = pl.BlockSpec(memory_space=pltpu.VMEM)
    smem = pl.BlockSpec(memory_space=pltpu.SMEM)
    V = pltpu.VMEM
    grads = pl.pallas_call(
        functools.partial(kernel, blocks, groups),
        out_shape=(
            jax.ShapeDtypeStruct((channels, length), BF16),
            jax.ShapeDtypeStruct((channels, length), BF16),
            jax.ShapeDtypeStruct((channels, length), BF16),
            jax.ShapeDtypeStruct((1, LANES), F32),
            jax.ShapeDtypeStruct((1, LANES), F32),
            jax.ShapeDtypeStruct((share_w, channels), F32),
        ),
        in_specs=[vmem] * 8 + [smem, vmem],
        out_specs=(vmem,) * 6,
        scratch_shapes=[
            V((half_count, row1, LANES), F32),
            V((half_count, row1, LANES), BF16),
            V((blocks, row1, LANES), BF16),
            V((blocks * row1, LANES), F32),
            V((share, 2 * blocks, LANES), F32),
            V((share, 2 * blocks, LANES), F32),
            V((rows, LANES), F32),
            V((rows, LANES), F32),
            V((blocks, LANES), F32),
            V((blocks, LANES), F32),
            V((rows, span + LANES), BF16),
            V((rows, span + LANES), BF16),
            V((span, 2 * LANES), BF16),
            V((span, 2 * LANES), BF16),
            V((2 * LANES, span), BF16),
            V((2 * LANES, span), BF16),
            V((half_count * row2, LANES), F32),
            V((half_count * row2, LANES), F32),
            V((channels, LANES), F32),
            V((channels, LANES), F32),
            V((channels, LANES), F32),
            V((groups, channels, LANES), BF16),
            V((LANES, width), BF16),
            V((1, LANES), F32),
            V((channels, LANES), BF16),
            V((groups, channels, LANES), BF16),
            V((channels, LANES), BF16),
            V((groups, channels, LANES), BF16),
            V((blocks, share_w // 2, LANES), BF16),
            V((blocks, share_w // 2, LANES), BF16),
            V((half_count, share, LANES), BF16),
            V((blocks, share, LANES), BF16),
            V((rows, LANES), F32),
            V((rows, span), BF16),
            V((LANES, (half_count + 1) * LANES), F32),
            V((half_count, LANES), F32),
            V((half_count * row1, LANES), F32),
            V((half_count, row1, LANES), BF16),
            V((half_count, row1, LANES), BF16),
            pltpu.SemaphoreType.DMA((8,)),
            pltpu.SemaphoreType.DMA((8,)),
        ],
        compiler_params=pltpu.CompilerParams(
            collective_id=0, has_side_effects=True, vmem_limit_bytes=48 << 20
        ),
    )(
        values.T,
        gate_inner.T,
        gate_outer.T,
        teacher.T,
        filter_one,
        filter_two,
        w_out.T,
        gene_ids.reshape(1, LANES),
        cell_lengths,
        table,
    )
    return (grads[0].T, grads[1].T, grads[2].T) + tuple(grads[3:])


def solution(mesh):
    blocks, groups = mesh.shape["seq"], mesh.shape["chan"]
    return jax.shard_map(
        functools.partial(per_device, blocks, groups),
        mesh=mesh,
        in_specs=(
            P("seq", "chan"),
            P("seq", "chan"),
            P("seq", "chan"),
            P("chan", "seq"),
            P("chan", "seq"),
            P("seq", "chan"),
            P(None, "chan"),
            P("seq"),
            P(),
            P(),
        ),
        out_specs=(
            P("seq", "chan"),
            P("seq", "chan"),
            P("seq", "chan"),
            P("chan", "seq"),
            P("chan", "seq"),
            P("seq", "chan"),
        ),
        check_vma=False,
    )
```

time: 560 us -> 82.5 us (0.15)
  waiting for transfers between devices: 281 us -> 0 us
  blocking collectives: 152 us -> 0 us
  Pallas kernels: 0 us -> 77.1 us
  starting transfers between devices: 60.3 us -> 0 us
  matrix products: 16.1 us -> 0 us
  local copies, waits for them, and re-layouts: 20.5 us -> 4.48 us
  between operations: 16.6 us -> 0.78 us
  other arithmetic: 8.36 us -> 0 us
    all_to_all x6 -> x0, blocking collectives: 117 us -> none  [the longest x5 99.4 us: spread_out(): lax.all_to_all(packed, 'seq', split_axis=0, concat_axis=1, tiled=True)]
    all_to_all x10 -> x0, waiting for transfers between devices: 117 us -> none  [the longest x7 83.6 us: bring_back(): lax.all_to_all(packed, 'seq', split_axis=1, concat_axis=0, tiled=True)]
    reduce_scatter x1 -> x0, waiting for transfers between devices: 91 us -> none  [project(): lax.psum_scatter(partial_w, 'seq', scatter_dimension=0, tiled=True)]
    pallas_call x0 -> x1, Pallas kernels: none -> 77.1 us  [per_device(): pl.pallas_call(functools.partial(kernel, blocks, groups), out_shape=(jax....]
    unnamed x3 -> x0, waiting for transfers between devices: 72.6 us -> none
    all_to_all x10 -> x0, starting transfers between devices: 60.2 us -> none  [the longest x7 33.4 us: bring_back(): lax.all_to_all(packed, 'seq', split_axis=1, concat_axis=0, tiled=True)]
    all_gather x1 -> x0, blocking collectives: 34.6 us -> none  [project(): gathered = lax.all_gather(pooled_in, 'chan', axis=1, tiled=True)]
    dot_general x35 -> x0, matrix products: 16.1 us -> none  [the longest x8 4.52 us: long_transform(): cos_part = jnp.dot(table_cos, stacked, precision=PRECISE)]
  transfers between devices with their start and end apart: 12 -> 0, of which waited for: 12 -> 0; matrix products, arithmetic and copies ran while one was open for 1% -> 0% of each run, Pallas kernels for 0% -> 0%
where the time goes in v1:
time: 82.5 us; the launch traced here: 82.4 us
  Pallas kernels  77.1 us (93%)
  local copies, waits for them, and re-layouts  4.48 us (5%)
    pallas_call x1, Pallas kernels, per_device(): pl.pallas_call(functools.partial(kernel, blocks, groups), out_shape=(jax....  77.1 us
    unnamed x24, local copies, waits for them, and re-layouts  3.48 us

profile of v1, /device:TPU:1, one launch (start us, length us, event | category | flops | bytes accessed | tf_op | source)
XLA Modules:
  0.0 82.4 jit_solution(7810789068345724983)
XLA Ops:
  0.6 0.0 copy-start
  0.6 0.0 copy-start.1
  0.7 0.0 copy-start.2
  0.7 0.0 copy-start.3
  0.7 0.0 copy-start.4
  0.7 0.0 copy-start.5
  0.7 0.0 copy-start.6
  0.7 0.0 copy-start.7
  0.7 0.0 copy-start.8
  0.7 1.0 %pad_bitcast_fusion.table = f32[200,128]{1,0:T(8,128)S(1)} fusion(f32[25426]{0:T(1024)} %param.19), kind=kLoop, calls=%fused_computation | loop fusion | bytes 204104 | tf_op jit(solution)/shard_map/reshape | solution.py:448
  1.7 0.0 copy-done
  1.7 0.0 copy-done.1
  1.7 0.0 copy-done.2
  1.8 0.0 copy-done.3
  1.8 0.0 copy-done.4
  1.8 0.0 copy-done.5
  1.8 0.0 copy-done.6
  1.8 0.0 copy-done.7
  1.8 0.0 copy-done.8
  1.8 77.1 %shard_map.145 = (bf16[64,128]{1,0:T(8,128)(2,1)S(1)}, bf16[64,128]{1,0:T(8,128)(2,1)S(1)}, bf16[64,128]{1,0:T(8,128)(2,1)S(1)}, f32[1,128]{1,0:T(1,128)S(1)}, f...) custom-call(bf16[64,128]{1,0:T(8,128)(2,1)S(1)} %bitcast.12, bf16[64,128]{1,0:T(8,128)(2,1)S(1)} %bitcast.13, ...), custom_call_target="tpu_custom_call" | custom-call | tf_op jit(solution)/shard_map/pallas_call | solution.py:452
  78.9 0.6 copy.22
  79.5 0.6 copy.23
  80.1 0.6 copy.24
  80.8 0.5 copy.25
  81.3 0.5 copy.26
  81.8 0.6 copy.27
Async XLA Ops:
  0.6 1.1 %copy-start = (bf16[1024,64]{0,1:T(8,128)(2,1)S(1)}, bf16[1024,64]{0,1:T(8,128)(2,1)}, u32[]{:S(2)}) copy-start(bf16[1024,64]{0,1:T(8,128)(2,1)} %param.16) | copy-start | bytes 393220
  0.6 1.1 %copy-start.1 = (bf16[128,64]{0,1:T(8,128)(2,1)S(1)}, bf16[128,64]{0,1:T(8,128)(2,1)}, u32[]{:S(2)}) copy-start(bf16[128,64]{0,1:T(8,128)(2,1)} %param.10) | copy-start | bytes 49156
  0.7 1.1 %copy-start.2 = (bf16[128,64]{0,1:T(8,128)(2,1)S(1)}, bf16[128,64]{0,1:T(8,128)(2,1)}, u32[]{:S(2)}) copy-start(bf16[128,64]{0,1:T(8,128)(2,1)} %param.11) | copy-start | bytes 49156
  0.7 1.1 %copy-start.3 = (bf16[128,64]{0,1:T(8,128)(2,1)S(1)}, bf16[128,64]{0,1:T(8,128)(2,1)}, u32[]{:S(2)}) copy-start(bf16[128,64]{0,1:T(8,128)(2,1)} %param.12) | copy-start | bytes 49156
  0.7 1.1 %copy-start.4 = (bf16[128,64]{0,1:T(8,128)(2,1)S(1)}, bf16[128,64]{0,1:T(8,128)(2,1)}, u32[]{:S(2)}) copy-start(bf16[128,64]{0,1:T(8,128)(2,1)} %param.15) | copy-start | bytes 49156
  0.7 1.1 %copy-start.5 = (f32[1,128]{1,0:T(1,128)S(1)}, f32[1,128]{1,0:T(1,128)}, u32[]{:S(2)}) copy-start(f32[1,128]{1,0:T(1,128)} %filter_one.1) | copy-start | bytes 1540
  0.7 1.1 %copy-start.6 = (f32[1,128]{1,0:T(1,128)S(1)}, f32[1,128]{1,0:T(1,128)}, u32[]{:S(2)}) copy-start(f32[1,128]{1,0:T(1,128)} %filter_two.1) | copy-start | bytes 1540
  0.7 1.1 %copy-start.7 = (s32[128]{0:T(128)S(1)}, s32[128]{0:T(128)}, u32[]{:S(2)}) copy-start(s32[128]{0:T(128)} %param.17) | copy-start | bytes 1540
  0.7 1.1 %copy-start.8 = (s32[4]{0:T(128)S(1)}, s32[4]{0:T(128)}, u32[]{:S(2)}) copy-start(s32[4]{0:T(128)} %cell_lengths.1) | copy-start | bytes 52

commit v2 on v1

v2 whole, which is shorter than its diff:
```python
import functools

import jax
import jax.numpy as jnp
from jax import lax
from jax.experimental import pallas as pl
from jax.experimental.pallas import tpu as pltpu
from jax.sharding import PartitionSpec as P

F32 = jnp.float32
BF16 = jnp.bfloat16
MESH = pl.DeviceIdType.MESH
HIGHEST = lax.Precision.HIGHEST
LANES = 128


def nn(left, right, precision=None):
    return lax.dot_general(
        left, right, (((1,), (0,)), ((), ())), precision=precision, preferred_element_type=F32
    )


def nt(left, right):
    return lax.dot_general(left, right, (((1,), (1,)), ((), ())), preferred_element_type=F32)


def tn(left, right, precision=None):
    return lax.dot_general(
        left, right, (((0,), (0,)), ((), ())), precision=precision, preferred_element_type=F32
    )


def split(value):
    high = value.astype(BF16)
    return high, (value - high.astype(F32)).astype(BF16)


def multiple(index, factor):
    return pl.multiple_of(index * factor, factor)


def kernel(
    blocks,
    groups,
    values,
    gate_inner,
    gate_outer,
    teacher,
    filter_one,
    filter_two,
    w_out,
    gene_ids,
    cell_lengths,
    table,
    out_values,
    out_inner,
    out_outer,
    out_one,
    out_two,
    out_w,
    stage,
    send1,
    recv1,
    flat1,
    pad,
    gate_c,
    conv_c,
    lags_one,
    lags_two,
    back_one,
    back_two,
    wide_one,
    wide_two,
    wide_back,
    toe_one,
    toe_two,
    upper_one,
    upper_two,
    total,
    send2,
    recv2,
    second_t,
    outer_t,
    teach_t,
    w_blocks,
    w_rows,
    token_w,
    pooled_t,
    pooled_all,
    dev_t,
    dev_all,
    gw_send,
    gw_recv,
    send5,
    recv5,
    cross,
    sums,
    flat6,
    send6,
    recv6,
    send_sem,
    recv_sem,
):
    half_count = blocks // 2
    channels = values.shape[0]
    share = channels // half_count
    rows = share * blocks
    own_rows = share * half_count
    row1 = send1.shape[1]
    row6 = send6.shape[1]
    span = wide_one.shape[1] // LANES
    steps = blocks // span
    shift = share * span
    s = lax.axis_index("seq")
    g = lax.axis_index("chan")
    half = lax.div(s, half_count)
    place = lax.rem(s, half_count)

    ring = half_count // 2
    near = [(turn, core) for turn in range(ring) for core in (0, 1)]
    near.sort(key=lambda at: -min(at[0], ring - at[0]))

    def place_at(turn, core):
        return jnp.bitwise_xor(jnp.bitwise_and(place + 2 * turn, half_count - 1), core)

    half_peers = [place_at(turn, core) for turn, core in near if turn or core]
    seq_peers = [(1 - half, place_at(turn, core)) for turn, core in near]
    seq_peers = seq_peers + [(half, peer) for peer in half_peers]
    chan_order = sorted(range(1, groups), key=lambda d: -(min(d // 4, 4 - d // 4) + d % 4))
    chan_peers = [jnp.bitwise_and(g + d, groups - 1) for d in chan_order]

    barrier = pltpu.get_barrier_semaphore()
    for other, peer in seq_peers:
        pl.semaphore_signal(
            barrier, inc=1, device_id={"seq": other * half_count + peer}, device_id_type=MESH
        )
    for peer in chan_peers:
        pl.semaphore_signal(barrier, inc=1, device_id={"chan": peer}, device_id_type=MESH)

    def remote(src, dst, index, device):
        pltpu.make_async_remote_copy(
            src_ref=src,
            dst_ref=dst,
            send_sem=send_sem.at[index],
            recv_sem=recv_sem.at[index],
            device_id=device,
            device_id_type=MESH,
        ).start()

    def to_seq(index, src_of, dst):
        for other, peer in seq_peers:
            remote(src_of(other, peer), dst, index, {"seq": other * half_count + peer})
        pltpu.make_async_copy(src_of(half, place), dst, recv_sem.at[index]).start()

    def to_half(index, src_of, dst):
        for peer in half_peers:
            remote(src_of(peer), dst, index, {"seq": half * half_count + peer})
        pltpu.make_async_copy(src_of(place), dst, recv_sem.at[index]).start()

    def to_chan(index, src_of, dst):
        for peer in chan_peers:
            remote(src_of(peer), dst, index, {"chan": peer})
        pltpu.make_async_copy(src_of(g), dst, recv_sem.at[index]).start()

    def arrived(index, ref):
        pltpu.make_async_copy(ref, ref, recv_sem.at[index]).wait()

    def sent(index, ref):
        pltpu.make_async_copy(ref, ref, send_sem.at[index]).wait()

    values_t = values[...].astype(F32)
    inner_t = gate_inner[...].astype(F32)
    high_one, low_one = split(filter_one[...])
    high_two, low_two = split(filter_two[...])
    filter_rows = jnp.concatenate(
        [high_one.astype(F32), low_one.astype(F32), high_two.astype(F32), low_two.astype(F32)], axis=0
    )
    for p in range(half_count):
        stage[p, 0:share, :] = values_t[p * share : (p + 1) * share]
        stage[p, share : 2 * share, :] = inner_t[p * share : (p + 1) * share]
        stage[p, 2 * share : 2 * share + 4, :] = filter_rows
        if 2 * share + 4 < row1:
            stage[p, 2 * share + 4 : row1, :] = jnp.zeros((row1 - 2 * share - 4, LANES), F32)
    send1[...] = stage[...].astype(BF16)
    pl.semaphore_wait(barrier, blocks + groups - 2)
    to_seq(0, lambda other, peer: send1.at[peer], recv1.at[s])
    to_chan(
        1,
        lambda peer: w_out.at[:, pl.ds(multiple(lax.div(peer, 2), LANES), LANES)],
        w_blocks.at[g],
    )

    outer_t[...] = gate_outer[...].astype(F32)
    teach_t[...] = teacher[...].astype(F32)
    ids = gene_ids[...]
    hot_rows = (
        lax.broadcasted_iota(jnp.int32, (table.shape[0], LANES), 0) == lax.shift_right_logical(ids, 7)
    ).astype(F32)
    picked = tn(table[...], hot_rows, HIGHEST)
    hot_lanes = lax.broadcasted_iota(jnp.int32, (LANES, LANES), 0) == jnp.bitwise_and(ids, 127)
    weight = jnp.sum(jnp.where(hot_lanes, picked, 0.0), axis=0, keepdims=True)
    token = s * LANES + lax.broadcasted_iota(jnp.int32, (1, LANES), 1)
    opening = token == 0
    start = cell_lengths[0]
    for cell in range(1, cell_lengths.shape[0]):
        opening = jnp.logical_or(opening, token == start)
        start = start + cell_lengths[cell]
    token_w[...] = jnp.where(opening, 0.0, weight)
    edge = pad.shape[0] - rows
    edge = edge // 2
    for first in (0, edge + rows):
        pad[first : first + edge, :] = jnp.zeros((edge, LANES), F32)
    empty = jnp.zeros((rows, span * LANES), BF16)
    wide_one[0:rows, :] = empty
    wide_two[0:rows, :] = empty
    wide_back[rows : 2 * rows, :] = empty

    row_iota = lax.broadcasted_iota(jnp.int32, (LANES, LANES), 0)
    lane_iota = lax.broadcasted_iota(jnp.int32, (LANES, LANES), 1)
    flip = (row_iota + lane_iota == LANES - 1).astype(BF16)
    row8 = lax.broadcasted_iota(jnp.int32, (8, LANES), 0)
    lane8 = lax.broadcasted_iota(jnp.int32, (8, LANES), 1)
    tiles = LANES // 8

    def staggered(block, first):
        return pltpu.roll(block, first, axis=1, stride=1, stride_axis=0)

    def turn(block, amount):
        return pltpu.roll(block, amount, axis=1) if amount else block

    def toeplitz_block(row, before, write, upper):
        base = staggered(jnp.broadcast_to(row, (8, LANES)), 1 if upper else 0)
        turned = [turn(base, 8 * j) for j in range(tiles)]
        for j in range(0, tiles, 2):
            pair = []
            for i in (j, j + 1):
                keep = lane8 <= row8 + 8 * i if upper else lane8 >= row8 + 8 * i
                pair.append(jnp.where(keep, turned[i], before[i]))
            high, low = split(jnp.concatenate(pair, axis=0))
            write(8 * j, high, low)
        return turned

    def toeplitz_loop(lags, toe):
        def body(m, before):
            def write(first, high, low):
                at = pl.ds(pl.multiple_of(m * LANES + first, 16), 16)
                toe[at, 0:LANES] = high
                toe[at, LANES : 2 * LANES] = low

            return tuple(toeplitz_block(lags[pl.ds(m, 1), :], before, write, True))

        lax.fori_loop(0, blocks, body, (jnp.zeros((8, LANES), F32),) * tiles)

    def toeplitz_step(lags, toe, step, before):
        for m in range(step * span, (step + 1) * span):

            def write(first, high, low):
                at = slice(m * LANES + first, m * LANES + first + 16)
                toe[at, 0:LANES] = high
                toe[at, LANES : 2 * LANES] = low

            before = toeplitz_block(lags[m : m + 1, :], before, write, False)
        return before

    def weights_of(toe, step):
        return toe[step * span * LANES : (step + 1) * span * LANES, :]

    def joined(product):
        return product[:, 0:LANES] + product[:, LANES : 2 * LANES]

    def widen(wide, first, direction):
        for j in range(span):
            at = edge + direction * share * j
            wide[first : first + rows, j * LANES : (j + 1) * LANES] = pad[at : at + rows, :].astype(BF16)

    own_at = pl.ds(multiple(half, own_rows), own_rows)
    arrived(0, recv1)
    flat1[...] = recv1[...].astype(F32).reshape(blocks * row1, LANES)

    def every(first):
        return flat1[pl.ds(first, blocks, stride=row1), :]

    lags_one[...] = every(2 * share) + every(2 * share + 1)
    lags_two[...] = every(2 * share + 2) + every(2 * share + 3)
    for c in range(share):
        pad[pl.ds(edge + c, blocks, stride=share), :] = every(c)
        gate_c[pl.ds(c, blocks, stride=share), :] = every(share + c)
    widen(wide_one, rows, -1)
    before = [jnp.zeros((8, LANES), F32)] * tiles
    for step in range(steps):
        before = toeplitz_step(lags_one, toe_one, step, before)
        part = nn(wide_one[rows : 2 * rows - shift * step, :], weights_of(toe_one, step))
        if step == 0:
            total[...] = part
        else:
            total[shift * step : rows, :] += part
    first_conv = joined(total[...])
    conv_c[...] = first_conv
    pad[edge : edge + rows, :] = gate_c[...] * first_conv
    widen(wide_two, rows, -1)
    before = [jnp.zeros((8, LANES), F32)] * tiles
    product = jnp.zeros((own_rows, 2 * LANES), F32)
    for step in range(steps):
        before = toeplitz_step(lags_two, toe_two, step, before)
        at = pl.multiple_of(rows + half * own_rows - shift * step, shift)
        product = product + nn(wide_two[pl.ds(at, own_rows), :], weights_of(toe_two, step))
    send2[...] = joined(product).reshape(half_count, share, LANES)
    to_half(2, lambda peer: send2.at[peer], recv2.at[place])

    back_two[...] = nn(every(2 * share + 2).astype(BF16), flip) + nn(every(2 * share + 3).astype(BF16), flip)
    toeplitz_loop(back_two, upper_two)
    arrived(1, w_blocks)
    stacked = w_blocks[...].astype(F32).reshape(groups * channels, LANES)
    w_rows[...] = stacked.T.astype(BF16)

    arrived(2, recv2)
    second_t[...] = recv2[...].reshape(channels, LANES)
    pooled_t[...] = (outer_t[...] * second_t[...]).astype(BF16)
    to_chan(3, lambda peer: pooled_t, pooled_all.at[g])
    back_one[...] = nn(every(2 * share).astype(BF16), flip) + nn(every(2 * share + 1).astype(BF16), flip)
    toeplitz_loop(back_one, upper_one)
    arrived(3, pooled_all)
    width = groups * channels
    pooled = pooled_all[...].reshape(width, LANES)
    output = nn(w_out[...], pooled)
    deviation = (token_w[...] * (output - teach_t[...])).astype(BF16)
    dev_t[...] = deviation
    to_chan(4, lambda peer: dev_t, dev_all.at[g])

    share_w = width // blocks
    half_w = share_w // 2
    parts = pooled.reshape(blocks, 2, half_w, LANES)
    left = jnp.concatenate(
        [parts[:, 0].reshape(blocks * half_w, LANES), parts[:, 1].reshape(blocks * half_w, LANES)], axis=1
    )
    blank = jnp.zeros_like(deviation)
    right = jnp.concatenate(
        [jnp.concatenate([deviation, blank], axis=1), jnp.concatenate([blank, deviation], axis=1)], axis=0
    )
    gw_send[...] = nt(left, right).reshape(blocks, half_w, LANES).astype(gw_send.dtype)
    to_seq(5, lambda other, peer: gw_send.at[other * half_count + peer], gw_recv.at[s])

    arrived(4, dev_all)
    back_outer = nn(
        w_rows[pl.ds(multiple(lax.rem(g, 2), channels), channels), :], dev_all[...].reshape(width, LANES)
    )
    back_second = back_outer * outer_t[...]
    send5[...] = back_second.astype(BF16).reshape(half_count, share, LANES)
    to_seq(6, lambda other, peer: send5.at[peer], recv5.at[s])
    out_outer[...] = (back_outer * second_t[...]).astype(BF16)

    arrived(6, recv5)
    signal = recv5[...].astype(F32).reshape(rows, LANES)
    pad[edge : edge + rows, :] = signal
    widen(wide_back, 0, 1)
    for step in range(steps):
        part = nn(wide_back[shift * step : rows, :], weights_of(upper_two, step))
        if step == 0:
            total[...] = part
        else:
            total[0 : rows - shift * step, :] += part
    back_inner = joined(total[...])
    back_first = back_inner * gate_c[...]
    pad[edge : edge + rows, :] = back_first
    conv_c[...] = back_inner * conv_c[...]
    widen(wide_back, 0, 1)
    product = jnp.zeros((own_rows, 2 * LANES), F32)
    for step in range(steps):
        at = pl.multiple_of(half * own_rows + shift * step, shift)
        product = product + nn(wide_back[pl.ds(at, own_rows), :], weights_of(upper_one, step))
    grad_values_c = joined(product)
    grad_inner_c = conv_c[own_at, :]
    for p in range(half_count):
        at = slice(p * share, (p + 1) * share)
        flat6[p * row6 : p * row6 + share, :] = grad_values_c[at]
        flat6[p * row6 + share : p * row6 + 2 * share, :] = grad_inner_c[at]

    def filter_grad(back, wide, column):
        turned = nt(flip, back.astype(BF16)).astype(BF16)
        for j in range(half_count // span):
            at = pl.multiple_of(rows - half * own_rows - shift * j, shift)
            cross[:, j * span * LANES : (j + 1) * span * LANES] = nn(turned, wide[pl.ds(at, rows), :])
        at = multiple(1 - half, own_rows)
        cross[:, half_count * LANES : (half_count + 1) * LANES] = nn(turned, wide[pl.ds(at, rows), 0:LANES])

        def block(m):
            return [
                turn(cross[8 * j : 8 * j + 8, m * LANES : (m + 1) * LANES], 8 * j) for j in range(tiles)
            ]

        def added(terms):
            while len(terms) > 1:
                terms = [a + b for a, b in zip(terms[::2], terms[1::2])]
            return terms[0]

        later = block(half_count)
        later = staggered(added([jnp.where(lane8 >= 8 * j, later[j], 0.0) for j in range(tiles)]), 0), later
        for m in range(half_count - 1, -1, -1):
            after_sum, after = later
            current = block(m)
            here = staggered(
                added([jnp.where(lane8 >= 8 * j, current[j], after[j]) for j in range(tiles)]), 0
            )
            sums[m : m + 1, :] = jnp.sum(jnp.where(lane8 >= row8, here, after_sum), axis=0, keepdims=True)
            later = here, current
        high, low = split(sums[...])
        flat6[pl.ds(column, half_count, stride=row6), :] = high.astype(F32)
        flat6[pl.ds(column + 1, half_count, stride=row6), :] = low.astype(F32)

    filter_grad(signal, wide_two, 2 * share + 2)
    filter_grad(back_first, wide_one, 2 * share)
    for c in range(2 * share + 4, row6):
        flat6[pl.ds(c, half_count, stride=row6), :] = jnp.zeros((half_count, LANES), F32)
    send6[...] = flat6[...].reshape(half_count, row6, LANES).astype(BF16)
    to_half(7, lambda peer: send6.at[peer], recv6.at[place])

    arrived(5, gw_recv)
    total_w = jnp.sum(gw_recv[...].astype(F32), axis=0)
    out_w[0:half_w, :] = total_w[:, 0:channels]
    out_w[half_w:share_w, :] = total_w[:, channels : 2 * channels]

    sent(0, recv1.at[pl.ds(0, blocks - 1)])
    sent(1, w_blocks.at[pl.ds(0, groups - 1)])
    sent(2, recv2.at[pl.ds(0, half_count - 1)])
    sent(3, pooled_all.at[pl.ds(0, groups - 1)])
    sent(4, dev_all.at[pl.ds(0, groups - 1)])
    sent(5, gw_recv.at[pl.ds(0, blocks - 1)])
    sent(6, recv5.at[pl.ds(0, blocks - 1)])
    arrived(7, recv6)
    flat6[...] = recv6[...].astype(F32).reshape(half_count * row6, LANES)
    for p in range(half_count):
        at = slice(p * share, (p + 1) * share)
        second_t[at, :] = flat6[p * row6 : p * row6 + share, :]
        outer_t[at, :] = flat6[p * row6 + share : p * row6 + 2 * share, :]
    out_values[...] = second_t[...].astype(BF16)
    out_inner[...] = outer_t[...].astype(BF16)
    lag_rows = []
    for column in (2 * share, 2 * share + 2):
        both = flat6[pl.ds(column, half_count, stride=row6), :] + flat6[
            pl.ds(column + 1, half_count, stride=row6), :
        ]
        lag_rows.append(jnp.sum(both, axis=0, keepdims=True))
    lag_rows.append(jnp.zeros((6, LANES), F32))
    ordered = nn(jnp.concatenate(lag_rows, axis=0), flip.astype(F32), HIGHEST)
    out_one[...] = ordered[0:1]
    out_two[...] = ordered[1:2]
    sent(7, recv6.at[pl.ds(0, half_count - 1)])


def hand_on(*refs):
    count = len(refs) // 2
    for source, target in zip(refs[:count], refs[count:]):
        target[...] = source[...]


def rounded(count, factor):
    return -(-count // factor) * factor


def per_device(
    blocks,
    groups,
    values,
    gate_inner,
    gate_outer,
    filter_one,
    filter_two,
    teacher,
    w_out,
    gene_ids,
    cell_lengths,
    gene_weights,
):
    length, channels = values.shape
    half_count = blocks // 2
    share = channels // half_count
    rows = share * blocks
    width = groups * channels
    share_w = width // blocks
    row1 = rounded(2 * share + 4, 16)
    span = max(1, 16 // share)
    vocab = gene_weights.shape[0]
    padded = rounded(vocab, 8 * LANES)
    table = jnp.pad(gene_weights, (0, padded - vocab)).reshape(padded // LANES, LANES)
    vmem = pl.BlockSpec(memory_space=pltpu.VMEM)
    smem = pl.BlockSpec(memory_space=pltpu.SMEM)
    V = pltpu.VMEM
    grads = pl.pallas_call(
        functools.partial(kernel, blocks, groups),
        out_shape=(
            jax.ShapeDtypeStruct((channels, length), BF16),
            jax.ShapeDtypeStruct((channels, length), BF16),
            jax.ShapeDtypeStruct((channels, length), BF16),
            jax.ShapeDtypeStruct((1, LANES), F32),
            jax.ShapeDtypeStruct((1, LANES), F32),
            jax.ShapeDtypeStruct((share_w, channels), F32),
        ),
        in_specs=[vmem] * 8 + [smem, vmem],
        out_specs=(vmem,) * 6,
        scratch_shapes=[
            V((half_count, row1, LANES), F32),
            V((half_count, row1, LANES), BF16),
            V((blocks, row1, LANES), BF16),
            V((blocks * row1, LANES), F32),
            V((rows + 32, LANES), F32),
            V((rows, LANES), F32),
            V((rows, LANES), F32),
            V((blocks, LANES), F32),
            V((blocks, LANES), F32),
            V((blocks, LANES), F32),
            V((blocks, LANES), F32),
            V((2 * rows, span * LANES), BF16),
            V((2 * rows, span * LANES), BF16),
            V((2 * rows, span * LANES), BF16),
            V((blocks * LANES, 2 * LANES), BF16),
            V((blocks * LANES, 2 * LANES), BF16),
            V((blocks * LANES, 2 * LANES), BF16),
            V((blocks * LANES, 2 * LANES), BF16),
            V((rows, 2 * LANES), F32),
            V((half_count, share, LANES), F32),
            V((half_count, share, LANES), F32),
            V((channels, LANES), F32),
            V((channels, LANES), F32),
            V((channels, LANES), F32),
            V((groups, channels, LANES), BF16),
            V((LANES, width), BF16),
            V((1, LANES), F32),
            V((channels, LANES), BF16),
            V((groups, channels, LANES), BF16),
            V((channels, LANES), BF16),
            V((groups, channels, LANES), BF16),
            V((blocks, share_w // 2, LANES), BF16),
            V((blocks, share_w // 2, LANES), BF16),
            V((half_count, share, LANES), BF16),
            V((blocks, share, LANES), BF16),
            V((LANES, (half_count + 1) * LANES), F32),
            V((half_count, LANES), F32),
            V((half_count * row1, LANES), F32),
            V((half_count, row1, LANES), BF16),
            V((half_count, row1, LANES), BF16),
            pltpu.SemaphoreType.DMA((8,)),
            pltpu.SemaphoreType.DMA((8,)),
        ],
        compiler_params=pltpu.CompilerParams(
            collective_id=0, has_side_effects=True, vmem_limit_bytes=48 << 20
        ),
    )(
        values.T,
        gate_inner.T,
        gate_outer.T,
        teacher.T,
        filter_one,
        filter_two,
        w_out.T,
        gene_ids.reshape(1, LANES),
        cell_lengths,
        table,
    )
    grads = pl.pallas_call(
        hand_on,
        out_shape=tuple(jax.ShapeDtypeStruct(grad.shape, grad.dtype) for grad in grads),
        in_specs=[vmem] * 6,
        out_specs=(vmem,) * 6,
        compiler_params=pltpu.CompilerParams(vmem_limit_bytes=1 << 20),
    )(*grads)
    return (grads[0].T, grads[1].T, grads[2].T) + tuple(grads[3:])


def solution(mesh):
    blocks, groups = mesh.shape["seq"], mesh.shape["chan"]
    return jax.shard_map(
        functools.partial(per_device, blocks, groups),
        mesh=mesh,
        in_specs=(
            P("seq", "chan"),
            P("seq", "chan"),
            P("seq", "chan"),
            P("chan", "seq"),
            P("chan", "seq"),
            P("seq", "chan"),
            P(None, "chan"),
            P("seq"),
            P(),
            P(),
        ),
        out_specs=(
            P("seq", "chan"),
            P("seq", "chan"),
            P("seq", "chan"),
            P("chan", "seq"),
            P("chan", "seq"),
            P("seq", "chan"),
        ),
        check_vma=False,
    )
```

time: 82.5 us -> 68.8 us (0.83)
  Pallas kernels: 77.1 us -> 66.8 us
  local copies, waits for them, and re-layouts: 4.48 us -> 1.04 us
    pallas_call x1, Pallas kernels: 77.1 us -> 66.2 us  [per_device(): pl.pallas_call(functools.partial(kernel, blocks, groups), out_shape=(jax....]
    unnamed x24 -> x18, local copies, waits for them, and re-layouts: 3.48 us -> 0.04 us
where the time goes in v2:
time: 68.8 us; the launch traced here: 68.6 us
  Pallas kernels  66.8 us (97%)
  local copies, waits for them, and re-layouts  1.04 us (2%)
  between operations  0.78 us (1%)
    pallas_call x1, Pallas kernels, per_device(): pl.pallas_call(functools.partial(kernel, blocks, groups), out_shape=(jax....  66.2 us

profile of v2, /device:TPU:1, one launch (start us, length us, event | category | flops | bytes accessed | tf_op | source)
XLA Modules:
  0.0 68.6 jit_solution(18024371549250279367)
XLA Ops:
  0.6 0.0 copy-start
  0.6 0.0 copy-start.1
  0.7 0.0 copy-start.2
  0.7 0.0 copy-start.3
  0.7 0.0 copy-start.4
  0.7 0.0 copy-start.5
  0.7 0.0 copy-start.6
  0.7 0.0 copy-start.7
  0.7 0.0 copy-start.8
  0.7 1.0 %pad_bitcast_fusion.table = f32[200,128]{1,0:T(8,128)S(1)} fusion(f32[25426]{0:T(1024)} %param.19), kind=kLoop, calls=%fused_computation | loop fusion | bytes 204104 | tf_op jit(solution)/shard_map/reshape | solution.py:484
  1.7 0.0 copy-done
  1.7 0.0 copy-done.1
  1.7 0.0 copy-done.2
  1.8 0.0 copy-done.3
  1.8 0.0 copy-done.4
  1.8 0.0 copy-done.5
  1.8 0.0 copy-done.6
  1.8 0.0 copy-done.7
  1.8 0.0 copy-done.8
  1.8 66.2 %shard_map.145 = (bf16[64,128]{1,0:T(8,128)(2,1)S(1)}, bf16[64,128]{1,0:T(8,128)(2,1)S(1)}, bf16[64,128]{1,0:T(8,128)(2,1)S(1)}, f32[1,128]{1,0:T(1,128)S(1)}, f...) custom-call(bf16[64,128]{1,0:T(8,128)(2,1)S(1)} %bitcast.12, bf16[64,128]{1,0:T(8,128)(2,1)S(1)} %bitcast.13, ...), custom_call_target="tpu_custom_call" | custom-call | tf_op jit(solution)/shard_map/pallas_call | solution.py:488
  68.0 0.6 shard_map.146
Async XLA Ops:
  0.6 1.1 %copy-start = (bf16[1024,64]{0,1:T(8,128)(2,1)S(1)}, bf16[1024,64]{0,1:T(8,128)(2,1)}, u32[]{:S(2)}) copy-start(bf16[1024,64]{0,1:T(8,128)(2,1)} %param.16) | copy-start | bytes 393220
  0.6 1.1 %copy-start.1 = (bf16[128,64]{0,1:T(8,128)(2,1)S(1)}, bf16[128,64]{0,1:T(8,128)(2,1)}, u32[]{:S(2)}) copy-start(bf16[128,64]{0,1:T(8,128)(2,1)} %param.10) | copy-start | bytes 49156
  0.7 1.1 %copy-start.2 = (bf16[128,64]{0,1:T(8,128)(2,1)S(1)}, bf16[128,64]{0,1:T(8,128)(2,1)}, u32[]{:S(2)}) copy-start(bf16[128,64]{0,1:T(8,128)(2,1)} %param.11) | copy-start | bytes 49156
  0.7 1.1 %copy-start.3 = (bf16[128,64]{0,1:T(8,128)(2,1)S(1)}, bf16[128,64]{0,1:T(8,128)(2,1)}, u32[]{:S(2)}) copy-start(bf16[128,64]{0,1:T(8,128)(2,1)} %param.12) | copy-start | bytes 49156
  0.7 1.1 %copy-start.4 = (bf16[128,64]{0,1:T(8,128)(2,1)S(1)}, bf16[128,64]{0,1:T(8,128)(2,1)}, u32[]{:S(2)}) copy-start(bf16[128,64]{0,1:T(8,128)(2,1)} %param.15) | copy-start | bytes 49156
  0.7 1.1 %copy-start.5 = (f32[1,128]{1,0:T(1,128)S(1)}, f32[1,128]{1,0:T(1,128)}, u32[]{:S(2)}) copy-start(f32[1,128]{1,0:T(1,128)} %filter_one.1) | copy-start | bytes 1540
  0.7 1.1 %copy-start.6 = (f32[1,128]{1,0:T(1,128)S(1)}, f32[1,128]{1,0:T(1,128)}, u32[]{:S(2)}) copy-start(f32[1,128]{1,0:T(1,128)} %filter_two.1) | copy-start | bytes 1540
  0.7 1.1 %copy-start.7 = (s32[128]{0:T(128)S(1)}, s32[128]{0:T(128)}, u32[]{:S(2)}) copy-start(s32[128]{0:T(128)} %param.17) | copy-start | bytes 1540
  0.7 1.1 %copy-start.8 = (s32[4]{0:T(128)S(1)}, s32[4]{0:T(128)}, u32[]{:S(2)}) copy-start(s32[4]{0:T(128)} %cell_lengths.1) | copy-start | bytes 52

commit v3 on v2

--- a/solution.py
+++ b/solution.py
@@ -51,7 +51,7 @@
     w_out,
     gene_ids,
     cell_lengths,
-    table,
+    gene_weights,
     out_values,
     out_inner,
     out_outer,
@@ -85,6 +85,7 @@
     w_blocks,
     w_rows,
     token_w,
+    table,
     pooled_t,
     pooled_all,
     dev_t,
@@ -184,14 +185,17 @@
     send1[...] = stage[...].astype(BF16)
     pl.semaphore_wait(barrier, blocks + groups - 2)
     to_seq(0, lambda other, peer: send1.at[peer], recv1.at[s])
-    to_chan(
-        1,
-        lambda peer: w_out.at[:, pl.ds(multiple(lax.div(peer, 2), LANES), LANES)],
-        w_blocks.at[g],
-    )
 
     outer_t[...] = gate_outer[...].astype(F32)
     teach_t[...] = teacher[...].astype(F32)
+    vocab = gene_weights.shape[0]
+    whole = vocab // LANES
+    table[whole - whole % 8 :, :] = jnp.zeros((table.shape[0] - whole + whole % 8, LANES), F32)
+    for line in range(whole):
+        table[line : line + 1, :] = gene_weights[pl.ds(line * LANES, LANES)].reshape(1, LANES)
+    if vocab % LANES:
+        rest = gene_weights[pl.ds(whole * LANES, vocab % LANES)].reshape(1, vocab % LANES)
+        table[whole : whole + 1, 0 : vocab % LANES] = rest
     ids = gene_ids[...]
     hot_rows = (
         lax.broadcasted_iota(jnp.int32, (table.shape[0], LANES), 0) == lax.shift_right_logical(ids, 7)
@@ -275,6 +279,11 @@
 
     own_at = pl.ds(multiple(half, own_rows), own_rows)
     arrived(0, recv1)
+    to_chan(
+        1,
+        lambda peer: w_out.at[:, pl.ds(multiple(lax.div(peer, 2), LANES), LANES)],
+        w_blocks.at[g],
+    )
     flat1[...] = recv1[...].astype(F32).reshape(blocks * row1, LANES)
 
     def every(first):
@@ -338,7 +347,6 @@
         [jnp.concatenate([deviation, blank], axis=1), jnp.concatenate([blank, deviation], axis=1)], axis=0
     )
     gw_send[...] = nt(left, right).reshape(blocks, half_w, LANES).astype(gw_send.dtype)
-    to_seq(5, lambda other, peer: gw_send.at[other * half_count + peer], gw_recv.at[s])
 
     arrived(4, dev_all)
     back_outer = nn(
@@ -347,6 +355,7 @@
     back_second = back_outer * outer_t[...]
     send5[...] = back_second.astype(BF16).reshape(half_count, share, LANES)
     to_seq(6, lambda other, peer: send5.at[peer], recv5.at[s])
+    to_seq(5, lambda other, peer: gw_send.at[other * half_count + peer], gw_recv.at[s])
     out_outer[...] = (back_outer * second_t[...]).astype(BF16)
 
     arrived(6, recv5)
@@ -480,8 +489,6 @@
     row1 = rounded(2 * share + 4, 16)
     span = max(1, 16 // share)
     vocab = gene_weights.shape[0]
-    padded = rounded(vocab, 8 * LANES)
-    table = jnp.pad(gene_weights, (0, padded - vocab)).reshape(padded // LANES, LANES)
     vmem = pl.BlockSpec(memory_space=pltpu.VMEM)
     smem = pl.BlockSpec(memory_space=pltpu.SMEM)
     V = pltpu.VMEM
@@ -525,6 +532,7 @@
             V((groups, channels, LANES), BF16),
             V((LANES, width), BF16),
             V((1, LANES), F32),
+            V((rounded(vocab, 8 * LANES) // LANES, LANES), F32),
             V((channels, LANES), BF16),
             V((groups, channels, LANES), BF16),
             V((channels, LANES), BF16),
@@ -554,7 +562,7 @@
         w_out.T,
         gene_ids.reshape(1, LANES),
         cell_lengths,
-        table,
+        gene_weights,
     )
     grads = pl.pallas_call(
         hand_on,

time: 68.8 us -> 70.1 us (1.019)
  local copies, waits for them, and re-layouts: 1.04 us -> 5.34 us
  Pallas kernels: 66.8 us -> 63.6 us
    unnamed x18 -> x20, local copies, waits for them, and re-layouts: 0.04 us -> 5.34 us
    pallas_call x1, Pallas kernels: 66.2 us -> 63 us  [per_device(): pl.pallas_call(functools.partial(kernel, blocks, groups), out_shape=(jax....]
    reshape x1 -> x0, local copies, waits for them, and re-layouts: 1 us -> none  [per_device(): jnp.pad(gene_weights, (0, padded - vocab)).reshape(padded // LANES, LANES)]
where the time goes in v3:
time: 70.1 us; the launch traced here: 69.7 us
  Pallas kernels  63.6 us (91%)
  local copies, waits for them, and re-layouts  5.34 us (8%)
    pallas_call x1, Pallas kernels, per_device(): pl.pallas_call(functools.partial(kernel, blocks, groups), out_shape=(jax....  63 us
    unnamed x20, local copies, waits for them, and re-layouts  5.34 us

profile of v3, /device:TPU:1, one launch (start us, length us, event | category | flops | bytes accessed | tf_op | source)
XLA Modules:
  0.0 69.7 jit_solution(14213796485064281219)
XLA Ops:
  0.6 0.0 copy-start.9
  0.6 0.0 copy-start.6
  0.7 0.0 copy-start.7
  0.7 0.0 copy-start.8
  0.7 0.6 copy-done.9
  1.3 0.0 copy-done.6
  1.3 0.0 copy-done.7
  1.3 0.0 copy-done.8
  1.3 0.0 copy-start
  1.3 0.9 %copy-done = bf16[1024,64]{0,1:T(8,128)(2,1)S(1)} copy-done((bf16[1024,64]{0,1:T(8,128)(2,1)S(1)}, bf16[1024,64]{0,1:T(8,128)(2,1)}, u32[]{:S(2)}) %copy-start) | copy-done | bytes 131096
  2.2 0.0 copy-start.1
  2.2 0.9 %copy-done.1 = f32[25426]{0:T(1024)S(1)} copy-done((f32[25426]{0:T(1024)S(1)}, f32[25426]{0:T(1024)}, u32[]{:S(2)}) %copy-start.1) | copy-done | bytes 101728
  3.1 0.0 copy-start.2
  3.1 0.7 %copy-done.2 = bf16[128,64]{0,1:T(8,128)(2,1)S(1)} copy-done((bf16[128,64]{0,1:T(8,128)(2,1)S(1)}, bf16[128,64]{0,1:T(8,128)(2,1)}, u32[]{:S(2)}) %copy-start.2) | copy-done | bytes 16408
  3.9 0.0 copy-start.3
  3.9 0.7 %copy-done.3 = bf16[128,64]{0,1:T(8,128)(2,1)S(1)} copy-done((bf16[128,64]{0,1:T(8,128)(2,1)S(1)}, bf16[128,64]{0,1:T(8,128)(2,1)}, u32[]{:S(2)}) %copy-start.3) | copy-done | bytes 16408
  4.6 0.0 copy-start.4
  4.6 0.7 %copy-done.4 = bf16[128,64]{0,1:T(8,128)(2,1)S(1)} copy-done((bf16[128,64]{0,1:T(8,128)(2,1)S(1)}, bf16[128,64]{0,1:T(8,128)(2,1)}, u32[]{:S(2)}) %copy-start.4) | copy-done | bytes 16408
  5.3 0.0 copy-start.5
  5.3 0.7 %copy-done.5 = bf16[128,64]{0,1:T(8,128)(2,1)S(1)} copy-done((bf16[128,64]{0,1:T(8,128)(2,1)S(1)}, bf16[128,64]{0,1:T(8,128)(2,1)}, u32[]{:S(2)}) %copy-start.5) | copy-done | bytes 16408
  6.0 63.0 %shard_map.145 = (bf16[64,128]{1,0:T(8,128)(2,1)S(1)}, bf16[64,128]{1,0:T(8,128)(2,1)S(1)}, bf16[64,128]{1,0:T(8,128)(2,1)S(1)}, f32[1,128]{1,0:T(1,128)S(1)}, f...) custom-call(bf16[64,128]{1,0:T(8,128)(2,1)S(1)} %bitcast.10, bf16[64,128]{1,0:T(8,128)(2,1)S(1)} %bitcast.11, ...), custom_call_target="tpu_custom_call" | custom-call | tf_op jit(solution)/shard_map/pallas_call | solution.py:495
  69.0 0.6 shard_map.146
Async XLA Ops:
  0.6 0.7 copy-start.9
  0.6 0.7 copy-start.6
  0.7 0.7 copy-start.7
  0.7 0.7 copy-start.8
  1.3 0.9 %copy-start = (bf16[1024,64]{0,1:T(8,128)(2,1)S(1)}, bf16[1024,64]{0,1:T(8,128)(2,1)}, u32[]{:S(2)}) copy-start(bf16[1024,64]{0,1:T(8,128)(2,1)} %param.16) | copy-start | bytes 393220
  2.2 0.9 %copy-start.1 = (f32[25426]{0:T(1024)S(1)}, f32[25426]{0:T(1024)}, u32[]{:S(2)}) copy-start(f32[25426]{0:T(1024)} %gene_weights.1) | copy-start | bytes 305116
  3.1 0.7 %copy-start.2 = (bf16[128,64]{0,1:T(8,128)(2,1)S(1)}, bf16[128,64]{0,1:T(8,128)(2,1)}, u32[]{:S(2)}) copy-start(bf16[128,64]{0,1:T(8,128)(2,1)} %param.10) | copy-start | bytes 49156
  3.9 0.7 %copy-start.3 = (bf16[128,64]{0,1:T(8,128)(2,1)S(1)}, bf16[128,64]{0,1:T(8,128)(2,1)}, u32[]{:S(2)}) copy-start(bf16[128,64]{0,1:T(8,128)(2,1)} %param.11) | copy-start | bytes 49156
  4.6 0.7 %copy-start.4 = (bf16[128,64]{0,1:T(8,128)(2,1)S(1)}, bf16[128,64]{0,1:T(8,128)(2,1)}, u32[]{:S(2)}) copy-start(bf16[128,64]{0,1:T(8,128)(2,1)} %param.12) | copy-start | bytes 49156
  5.3 0.7 %copy-start.5 = (bf16[128,64]{0,1:T(8,128)(2,1)S(1)}, bf16[128,64]{0,1:T(8,128)(2,1)}, u32[]{:S(2)}) copy-start(bf16[128,64]{0,1:T(8,128)(2,1)} %param.15) | copy-start | bytes 49156

commit v4 on v3

--- a/solution.py
+++ b/solution.py
@@ -42,6 +42,22 @@
 def kernel(
     blocks,
     groups,
+    values_in,
+    inner_in,
+    outer_in,
+    teacher_in,
+    one_in,
+    two_in,
+    w_in,
+    ids_in,
+    lengths_in,
+    weights_in,
+    out_values,
+    out_inner,
+    out_outer,
+    out_one,
+    out_two,
+    out_w,
     values,
     gate_inner,
     gate_outer,
@@ -52,12 +68,6 @@
     gene_ids,
     cell_lengths,
     gene_weights,
-    out_values,
-    out_inner,
-    out_outer,
-    out_one,
-    out_two,
-    out_w,
     stage,
     send1,
     recv1,
@@ -101,7 +111,27 @@
     recv6,
     send_sem,
     recv_sem,
+    fetch_sem,
 ):
+    fetches = [
+        pltpu.make_async_copy(source, target, fetch_sem.at[index])
+        for index, (source, target) in enumerate(
+            [
+                (values_in, values),
+                (inner_in, gate_inner),
+                (one_in, filter_one),
+                (two_in, filter_two),
+                (outer_in, gate_outer),
+                (teacher_in, teacher),
+                (ids_in, gene_ids),
+                (lengths_in, cell_lengths),
+                (weights_in, gene_weights),
+                (w_in, w_out),
+            ]
+        )
+    ]
+    for fetch in fetches:
+        fetch.start()
     half_count = blocks // 2
     channels = values.shape[0]
     share = channels // half_count
@@ -169,6 +199,8 @@
     def sent(index, ref):
         pltpu.make_async_copy(ref, ref, send_sem.at[index]).wait()
 
+    for fetch in fetches[:4]:
+        fetch.wait()
     values_t = values[...].astype(F32)
     inner_t = gate_inner[...].astype(F32)
     high_one, low_one = split(filter_one[...])
@@ -186,6 +218,8 @@
     pl.semaphore_wait(barrier, blocks + groups - 2)
     to_seq(0, lambda other, peer: send1.at[peer], recv1.at[s])
 
+    for fetch in fetches[4:]:
+        fetch.wait()
     outer_t[...] = gate_outer[...].astype(F32)
     teach_t[...] = teacher[...].astype(F32)
     vocab = gene_weights.shape[0]
@@ -490,7 +524,6 @@
     span = max(1, 16 // share)
     vocab = gene_weights.shape[0]
     vmem = pl.BlockSpec(memory_space=pltpu.VMEM)
-    smem = pl.BlockSpec(memory_space=pltpu.SMEM)
     V = pltpu.VMEM
     grads = pl.pallas_call(
         functools.partial(kernel, blocks, groups),
@@ -502,9 +535,19 @@
             jax.ShapeDtypeStruct((1, LANES), F32),
             jax.ShapeDtypeStruct((share_w, channels), F32),
         ),
-        in_specs=[vmem] * 8 + [smem, vmem],
+        in_specs=[pl.BlockSpec(memory_space=pltpu.HBM)] * 10,
         out_specs=(vmem,) * 6,
         scratch_shapes=[
+            V((channels, length), BF16),
+            V((channels, length), BF16),
+            V((channels, length), BF16),
+            V((channels, length), BF16),
+            V((1, LANES), F32),
+            V((1, LANES), F32),
+            V((channels, width), BF16),
+            V((1, LANES), jnp.int32),
+            pltpu.SMEM(cell_lengths.shape, jnp.int32),
+            V((vocab,), F32),
             V((half_count, row1, LANES), F32),
             V((half_count, row1, LANES), BF16),
             V((blocks, row1, LANES), BF16),
@@ -548,21 +591,27 @@
             V((half_count, row1, LANES), BF16),
             pltpu.SemaphoreType.DMA((8,)),
             pltpu.SemaphoreType.DMA((8,)),
+            pltpu.SemaphoreType.DMA((10,)),
         ],
         compiler_params=pltpu.CompilerParams(
             collective_id=0, has_side_effects=True, vmem_limit_bytes=48 << 20
         ),
     )(
-        values.T,
-        gate_inner.T,
-        gate_outer.T,
-        teacher.T,
-        filter_one,
-        filter_two,
-        w_out.T,
-        gene_ids.reshape(1, LANES),
-        cell_lengths,
-        gene_weights,
+        *(
+            pltpu.with_memory_space_constraint(operand, pltpu.HBM)
+            for operand in (
+                values.T,
+                gate_inner.T,
+                gate_outer.T,
+                teacher.T,
+                filter_one,
+                filter_two,
+                w_out.T,
+                gene_ids.reshape(1, LANES),
+                cell_lengths,
+                gene_weights,
+            )
+        )
     )
     grads = pl.pallas_call(
         hand_on,

time: 70.1 us -> 64.1 us (0.914)
  local copies, waits for them, and re-layouts: 5.34 us -> 0 us
    unnamed x20 -> x0, local copies, waits for them, and re-layouts: 5.34 us -> none
where the time goes in v4:
time: 64.1 us; the launch traced here: 63.9 us
  Pallas kernels  63.2 us (99%)
    pallas_call x1, Pallas kernels, per_device(): pl.pallas_call(functools.partial(kernel, blocks, groups), out_shape=(jax....  62.6 us

profile of v4, /device:TPU:1, one launch (start us, length us, event | category | flops | bytes accessed | tf_op | source)
XLA Modules:
  0.0 63.9 jit_solution(15363638105517223894)
XLA Ops:
  0.6 62.6 %shard_map.145 = (bf16[64,128]{1,0:T(8,128)(2,1)S(1)}, bf16[64,128]{1,0:T(8,128)(2,1)S(1)}, bf16[64,128]{1,0:T(8,128)(2,1)S(1)}, f32[1,128]{1,0:T(1,128)S(1)}, f...) custom-call(bf16[64,128]{1,0:T(8,128)(2,1)} %bitcast.10, bf16[64,128]{1,0:T(8,128)(2,1)} %bitcast.11, bf16[64,128]{1,0:T(8,128)(2,1)} %bitcast.12, ...), custom_call_target="tpu_custom_call" | custom-call | tf_op jit(solution)/shard_map/pallas_call | solution.py:528
  63.2 0.6 shard_map.146
